TPU v7x, 32 devices: a whole 2x2x4 slice. The times are simulated.
32 devices in a mesh: ctx: 8 (over z, x), wsh: 4 (over y, core).
Axes of the slice: x: 2, y: 2, z: 4, core: 2. Of those that a mesh axis runs over, the one named last changes fastest.
Arguments:
- layer_input: bfloat16 [4, 2048, 1536], P('wsh', 'ctx'), may hold values from -6 to 6
- attention_gain: bfloat16 [1536], P('wsh'), may hold values from 0.099609375 to 1.8984375
- query_weight: bfloat16 [1536, 1536], P('wsh'), may hold values from -0.15625 to 0.15625
- key_matrix: bfloat16 [1536, 512], P('wsh'), may hold values from -0.15625 to 0.15625
- value_matrix: bfloat16 [1536, 512], P('wsh'), may hold values from -0.15625 to 0.15625
- output_weight: bfloat16 [1536, 1536], P('wsh'), may hold values from -1.25 to 1.25
- expert_gain: bfloat16 [1536], P('wsh'), may hold values from 0.099609375 to 1.8984375
- router_weight: bfloat16 [1536, 16], P('wsh'), may hold values from -0.078125 to 0.078125
- expert_inner: bfloat16 [16, 1536, 1024], P('ctx', 'wsh'), may hold values from -0.15625 to 0.15625
- expert_outer: bfloat16 [16, 512, 1536], P('ctx', 'wsh'), may hold values from -0.75 to 0.75
- document_lengths: int32 [4, 4], P('wsh'), may hold values from 1 to 1024, 1792 in all within a row
- token_places: int32 [4, 2048], P('wsh'), may hold values from 0 to 2047, each once within a row
- expert_routes: int32 [4, 2048, 8], P('wsh', 'ctx'), may hold values from 0 to 15, all different within a row; in each aligned block of 256 rows (0 to 255, 256 to 511, ..., all dimensions but the last counted through in order) at most 192 rows name the same one
- cotangent: bfloat16 [4, 2048, 1536], P('wsh', 'ctx'), may hold values from -6 to 6
Outputs:
- layer_output: bfloat16 [4, 2048, 1536], P('wsh', 'ctx')
- input_gradient: float32 [4, 2048, 1536], P('wsh', 'ctx')
- attention_gain_gradient: float32 [1536], P('wsh')
- query_weight_gradient: float32 [1536, 1536], P('wsh')
- key_weight_gradient: float32 [1536, 512], P('wsh')
- value_weight_gradient: float32 [1536, 512], P('wsh')
- output_weight_gradient: float32 [1536, 1536], P('wsh')
- expert_gain_gradient: float32 [1536], P('wsh')
- router_weight_gradient: float32 [1536, 16], P('wsh')
- expert_inner_gradient: float32 [16, 1536, 1024], P('ctx', 'wsh')
- expert_outer_gradient: float32 [16, 512, 1536], P('ctx', 'wsh')
Inputs may be any that keep to these rules, and one draw needn't show every extreme that they name: `document_lengths`: each row holds the lengths of the 4 documents of one group in order; they sum to 1792, the longest is exactly 1024, and places from that sum on are pads. `token_places`: each row is a permutation of the places of one group. `expert_routes`: each token names 8 different experts. Among the 256 tokens of one device (aligned blocks of rows) no expert is named more than 192 times, a bound that some block reaches.
All inputs are finite; a program needn't handle non-finite values.
Results may differ from a plain program's by a relative error of at most 0.025.
Values may be sent and summed in bfloat16 or wider, within the bound.
A program may use at most 192 MiB of HBM per device.

v0:
```python
import math

import jax
import jax.numpy as jnp
from jax import lax
from jax.sharding import PartitionSpec as P

QUERY_HEADS = 24
KEY_HEADS = 8
HEAD_SIZE = 64
EXPERT_H = 512
TOPK = 8
EXP_DEV = 2
SEQS = 4


EPS = 1e-05
THETA = 10000.0
MASK_FILL = -1e30


def rms_inverse(matrix):
    return lax.rsqrt(jnp.mean(matrix * matrix, axis=-1, keepdims=True) + EPS)


def locate(lengths_row, places_row):
    segment_ends = jnp.cumsum(lengths_row)
    beyond = (places_row[:, None] >= segment_ends[None, :]).astype(jnp.int32)
    documents = jnp.sum(beyond, axis=1)
    offsets = places_row - jnp.sum(beyond * lengths_row[None, :], axis=1)
    return (documents, offsets)


def angles_for(offsets):
    halfway = HEAD_SIZE // 2
    frequency = THETA ** (-2.0 * jnp.arange(halfway, dtype=jnp.float32) / HEAD_SIZE)
    angles = offsets.astype(jnp.float32)[:, None] * frequency[None, :]
    return (jnp.cos(angles)[:, None, :], jnp.sin(angles)[:, None, :])


def apply_rotation(matrix, cosine_rows, sine_table):
    halfway = matrix.shape[-1] // 2
    former = matrix[..., :halfway]
    latter = matrix[..., halfway:]
    return jnp.concatenate(
        [former * cosine_rows - latter * sine_table, latter * cosine_rows + former * sine_table],
        axis=-1,
    )


def reverse_rotation(matrix, cosine_rows, sine_table):
    halfway = matrix.shape[-1] // 2
    former = matrix[..., :halfway]
    latter = matrix[..., halfway:]
    return jnp.concatenate(
        [former * cosine_rows + latter * sine_table, latter * cosine_rows - former * sine_table],
        axis=-1,
    )


def visible_mask(query_documents, query_places, key_documents, key_places):
    same_doc = (query_documents[:, None] == key_documents[None, :]) & (
        query_documents[:, None] < SEQS
    )
    causal = key_places[None, :] <= query_places[:, None]
    return same_doc & causal | (key_places[None, :] == query_places[:, None])


def norm_backward(matrix, inverse, gains, gradients):
    scaled = gradients * gains
    gain_grad = jnp.sum(gradients * matrix * inverse, axis=0)
    input_back = inverse * scaled - matrix * inverse * inverse * inverse * jnp.mean(
        scaled * matrix, axis=-1, keepdims=True
    )
    return (gain_grad, input_back)


def on_device(
    layer_input,
    attention_gain,
    query_weight,
    key_matrix,
    value_matrix,
    output_weight,
    expert_gain,
    router_weight,
    expert_inner,
    expert_outer,
    document_lengths,
    token_places,
    expert_routes,
    cotangent,
):
    group_devices = lax.axis_size("ctx")
    ctx_index = lax.axis_index("ctx")
    token_rows = layer_input.shape[1]
    model_width = layer_input.shape[2]
    experts = router_weight.shape[1]
    capacity = 3 * token_rows * TOPK // (2 * experts)
    group_rows = token_rows * group_devices
    heads_per_group = QUERY_HEADS // KEY_HEADS
    key_value_width = KEY_HEADS * HEAD_SIZE
    scale = HEAD_SIZE ** (-0.5)
    (
        gain_one,
        gain_two,
        whole_query,
        whole_key,
        whole_value,
        whole_output,
        whole_router,
        whole_inner,
        whole_outer,
    ) = (
        lax.all_gather(attention_gain, "wsh", axis=0, tiled=True),
        lax.all_gather(expert_gain, "wsh", axis=0, tiled=True),
        lax.all_gather(query_weight, "wsh", axis=0, tiled=True),
        lax.all_gather(key_matrix, "wsh", axis=0, tiled=True),
        lax.all_gather(value_matrix, "wsh", axis=0, tiled=True),
        lax.all_gather(output_weight, "wsh", axis=0, tiled=True),
        lax.all_gather(router_weight, "wsh", axis=0, tiled=True),
        lax.all_gather(expert_inner, "wsh", axis=1, tiled=True),
        lax.all_gather(expert_outer, "wsh", axis=1, tiled=True),
    )
    gain_one = gain_one.astype(jnp.float32)
    gain_two = gain_two.astype(jnp.float32)
    places_all = token_places[0]
    key_documents, key_offsets = locate(document_lengths[0], places_all)
    first_row = ctx_index * token_rows
    query_places = lax.dynamic_slice_in_dim(places_all, first_row, token_rows)
    query_documents = lax.dynamic_slice_in_dim(key_documents, first_row, token_rows)
    query_offsets = lax.dynamic_slice_in_dim(key_offsets, first_row, token_rows)
    cosine_rows, sine_table = angles_for(query_offsets)
    inputs_f = layer_input[0].astype(jnp.float32)
    inverse_one = rms_inverse(inputs_f)
    normed_one = (inputs_f * inverse_one * gain_one).astype(jnp.bfloat16)
    query_pre = jnp.dot(normed_one, whole_query, preferred_element_type=jnp.float32)
    key_unrotated = jnp.dot(normed_one, whole_key, preferred_element_type=jnp.float32)
    value_projected = jnp.dot(normed_one, whole_value, preferred_element_type=jnp.float32)
    rows_of_queries = apply_rotation(
        query_pre.reshape(token_rows, QUERY_HEADS, HEAD_SIZE), cosine_rows, sine_table
    ).astype(jnp.bfloat16)
    rows_of_keys = (
        apply_rotation(
            key_unrotated.reshape(token_rows, KEY_HEADS, HEAD_SIZE), cosine_rows, sine_table
        )
        .astype(jnp.bfloat16)
        .reshape(token_rows, key_value_width)
    )
    rows_of_values = value_projected.astype(jnp.bfloat16)
    all_keys, all_values = (
        lax.all_gather(rows_of_keys, "ctx", axis=0, tiled=True),
        lax.all_gather(rows_of_values, "ctx", axis=0, tiled=True),
    )
    heads_of_queries = rows_of_queries.reshape(
        token_rows, KEY_HEADS, heads_per_group, HEAD_SIZE
    ).transpose(1, 2, 0, 3)
    rows_per_block = math.gcd(group_rows, 512)
    count_blocks = group_rows // rows_per_block

    def forward_step(state, blocks):
        running_max, running_sum, accumulated = state
        key_tile, value_tile, doc_block, place_block = blocks
        scores = (
            jnp.einsum(
                "grtd,kgd->grtk",
                heads_of_queries,
                key_tile.reshape(rows_per_block, KEY_HEADS, HEAD_SIZE),
                preferred_element_type=jnp.float32,
            )
            * scale
        )
        visible = visible_mask(query_documents, query_places, doc_block, place_block)
        scores = jnp.where(visible, scores, MASK_FILL)
        new_max = jnp.maximum(running_max, jnp.max(scores, axis=-1))
        weights = jnp.where(visible, jnp.exp(scores - new_max[..., None]), 0.0)
        factor = jnp.exp(running_max - new_max)
        running_sum = running_sum * factor + jnp.sum(weights, axis=-1)
        accumulated = accumulated * factor[..., None] + jnp.einsum(
            "grtk,kgd->grtd",
            weights.astype(jnp.bfloat16),
            value_tile.reshape(rows_per_block, KEY_HEADS, HEAD_SIZE),
            preferred_element_type=jnp.float32,
        )
        return ((new_max, running_sum, accumulated), None)

    start_state = (
        jnp.full((KEY_HEADS, heads_per_group, token_rows), MASK_FILL, jnp.float32),
        jnp.zeros((KEY_HEADS, heads_per_group, token_rows), jnp.float32),
        jnp.zeros((KEY_HEADS, heads_per_group, token_rows, HEAD_SIZE), jnp.float32),
    )
    forward_blocks = (
        all_keys.reshape(count_blocks, rows_per_block, key_value_width),
        all_values.reshape(count_blocks, rows_per_block, key_value_width),
        key_documents.reshape(count_blocks, rows_per_block),
        places_all.reshape(count_blocks, rows_per_block),
    )
    (running_max, running_sum, accumulated), leftover = lax.scan(
        forward_step, start_state, forward_blocks
    )
    attended_heads = accumulated / running_sum[..., None]
    log_total = running_max + jnp.log(running_sum)
    attended = (
        attended_heads.transpose(2, 0, 1, 3)
        .reshape(token_rows, QUERY_HEADS * HEAD_SIZE)
        .astype(jnp.bfloat16)
    )
    residual = inputs_f + jnp.dot(attended, whole_output, preferred_element_type=jnp.float32)
    inverse_two = rms_inverse(residual)
    normed_two = (residual * inverse_two * gain_two).astype(jnp.bfloat16)
    logits = jnp.dot(normed_two, whole_router, preferred_element_type=jnp.float32)
    routes_here = expert_routes[0]
    expert_ids = jnp.arange(experts, dtype=jnp.int32)
    route_picks = (routes_here[:, :, None] == expert_ids[None, None, :]).astype(jnp.float32)
    chosen = jnp.sum(route_picks * logits[:, None, :], axis=-1)
    gate_values = jax.nn.softmax(chosen, axis=-1)
    flat_routes = routes_here.reshape(-1)
    route_marks = (flat_routes[:, None] == expert_ids[None, :]).astype(jnp.int32)
    earlier = jnp.sum((jnp.cumsum(route_marks, axis=0) - route_marks) * route_marks, axis=1)
    slot_index = flat_routes * capacity + earlier
    slot_shape = (group_devices, EXP_DEV, capacity, model_width)
    empty_slots = jnp.zeros((experts * capacity, model_width), jnp.bfloat16)
    send_rows = (
        empty_slots.at[slot_index].set(jnp.repeat(normed_two, TOPK, axis=0)).reshape(slot_shape)
    )
    received = lax.all_to_all(send_rows, "ctx", split_axis=0, concat_axis=0, tiled=True)
    gate_up = jnp.einsum(
        "sxcd,xdf->sxcf", received, whole_inner, preferred_element_type=jnp.float32
    )
    gate_part = gate_up[..., :EXPERT_H]
    up_part = gate_up[..., EXPERT_H:]
    silu_gate = jax.nn.silu(gate_part)
    hidden = (silu_gate * up_part).astype(jnp.bfloat16)
    expert_result = jnp.einsum(
        "sxcf,xfd->sxcd", hidden, whole_outer, preferred_element_type=jnp.float32
    ).astype(jnp.bfloat16)
    returned = lax.all_to_all(expert_result, "ctx", split_axis=0, concat_axis=0, tiled=True)
    picked = (
        returned.reshape(experts * capacity, model_width)[slot_index]
        .reshape(token_rows, TOPK, model_width)
        .astype(jnp.float32)
    )
    mixture = jnp.sum(gate_values[..., None] * picked, axis=1)
    layer_output = (residual + mixture).astype(jnp.bfloat16)
    out_grad = cotangent[0].astype(jnp.float32)
    gate_grad = jnp.sum(out_grad[:, None, :] * picked, axis=-1)
    chosen_grad = gate_values * (
        gate_grad - jnp.sum(gate_values * gate_grad, axis=-1, keepdims=True)
    )
    logit_grad = jnp.sum(route_picks * chosen_grad[..., None], axis=1).astype(jnp.bfloat16)
    router_grad = jnp.dot(normed_two.T, logit_grad, preferred_element_type=jnp.float32)
    normed_two_grad = jnp.dot(logit_grad, whole_router.T, preferred_element_type=jnp.float32)
    route_grad = (
        (gate_values[..., None] * out_grad[:, None, :])
        .astype(jnp.bfloat16)
        .reshape(token_rows * TOPK, model_width)
    )
    send_grads = empty_slots.at[slot_index].set(route_grad).reshape(slot_shape)
    result_grad = lax.all_to_all(send_grads, "ctx", split_axis=0, concat_axis=0, tiled=True)
    outer_grad = jnp.einsum(
        "sxcf,sxcd->xfd", hidden, result_grad, preferred_element_type=jnp.float32
    )
    hidden_grad = jnp.einsum(
        "sxcd,xfd->sxcf", result_grad, whole_outer, preferred_element_type=jnp.float32
    )
    sigmoid = jax.nn.sigmoid(gate_part)
    inner_rows = jnp.concatenate(
        [
            hidden_grad * up_part * sigmoid * (1.0 + gate_part * (1.0 - sigmoid)),
            hidden_grad * silu_gate,
        ],
        axis=-1,
    ).astype(jnp.bfloat16)
    inner_grad = jnp.einsum(
        "sxcd,sxcf->xdf", received, inner_rows, preferred_element_type=jnp.float32
    )
    row_grads = jnp.einsum(
        "sxcf,xdf->sxcd", inner_rows, whole_inner, preferred_element_type=jnp.float32
    ).astype(jnp.bfloat16)
    back_rows = lax.all_to_all(row_grads, "ctx", split_axis=0, concat_axis=0, tiled=True)
    normed_two_grad = normed_two_grad + jnp.sum(
        back_rows.reshape(experts * capacity, model_width)[slot_index]
        .reshape(token_rows, TOPK, model_width)
        .astype(jnp.float32),
        axis=1,
    )
    gain_two_grad, residual_back = norm_backward(residual, inverse_two, gain_two, normed_two_grad)
    residual_grad = out_grad + residual_back
    branch_grad = residual_grad.astype(jnp.bfloat16)
    output_grad = jnp.dot(attended.T, branch_grad, preferred_element_type=jnp.float32)
    attended_gradient = jnp.dot(
        branch_grad, whole_output.T, preferred_element_type=jnp.float32
    ).astype(jnp.bfloat16)
    head_gradients = attended_gradient.reshape(
        token_rows, KEY_HEADS, heads_per_group, HEAD_SIZE
    ).transpose(1, 2, 0, 3)
    row_delta = jnp.sum(head_gradients.astype(jnp.float32) * attended_heads, axis=-1)
    query_gradient = jnp.zeros((KEY_HEADS, heads_per_group, token_rows, HEAD_SIZE), jnp.float32)
    piece_rows = all_keys.shape[0]
    block_length = math.gcd(piece_rows, 512)
    piece_blocks = piece_rows // block_length
    back_blocks = (
        all_keys.reshape(piece_blocks, block_length, key_value_width),
        all_values.reshape(piece_blocks, block_length, key_value_width),
        key_documents.reshape(piece_blocks, block_length),
        places_all.reshape(piece_blocks, block_length),
    )

    def back_step(query_sum, blocks):
        key_tile, value_tile, doc_block, place_block = blocks
        heads_of_keys = key_tile.reshape(block_length, KEY_HEADS, HEAD_SIZE)
        heads_of_values = value_tile.reshape(block_length, KEY_HEADS, HEAD_SIZE)
        scores = (
            jnp.einsum(
                "grtd,kgd->grtk",
                heads_of_queries,
                heads_of_keys,
                preferred_element_type=jnp.float32,
            )
            * scale
        )
        visible = visible_mask(query_documents, query_places, doc_block, place_block)
        attention_probs = jnp.exp(jnp.where(visible, scores - log_total[..., None], MASK_FILL))
        prob_grad = jnp.einsum(
            "grtd,kgd->grtk", head_gradients, heads_of_values, preferred_element_type=jnp.float32
        )
        score_grad = (attention_probs * (prob_grad - row_delta[..., None])).astype(jnp.bfloat16)
        value_part = jnp.einsum(
            "grtk,grtd->kgd",
            attention_probs.astype(jnp.bfloat16),
            head_gradients,
            preferred_element_type=jnp.float32,
        )
        key_part = (
            jnp.einsum(
                "grtk,grtd->kgd", score_grad, heads_of_queries, preferred_element_type=jnp.float32
            )
            * scale
        )
        query_sum = (
            query_sum
            + jnp.einsum(
                "grtk,kgd->grtd", score_grad, heads_of_keys, preferred_element_type=jnp.float32
            )
            * scale
        )
        return (
            query_sum,
            (
                key_part.reshape(block_length, key_value_width),
                value_part.reshape(block_length, key_value_width),
            ),
        )

    query_gradient, (key_parts, value_parts) = lax.scan(back_step, query_gradient, back_blocks)
    key_grad = key_parts.reshape(piece_rows, key_value_width)
    value_grad = value_parts.reshape(piece_rows, key_value_width)
    query_gradient, key_grad, value_grad = (query_gradient, key_grad, value_grad)
    local_keys, value_local = (
        lax.psum_scatter(
            key_grad.astype(jnp.bfloat16), "ctx", scatter_dimension=0, tiled=True
        ).astype(jnp.float32),
        lax.psum_scatter(
            value_grad.astype(jnp.bfloat16), "ctx", scatter_dimension=0, tiled=True
        ).astype(jnp.float32),
    )
    query_pre_grad = (
        reverse_rotation(
            query_gradient.transpose(2, 0, 1, 3).reshape(token_rows, QUERY_HEADS, HEAD_SIZE),
            cosine_rows,
            sine_table,
        )
        .reshape(token_rows, QUERY_HEADS * HEAD_SIZE)
        .astype(jnp.bfloat16)
    )
    key_pre_grad = (
        reverse_rotation(
            local_keys.reshape(token_rows, KEY_HEADS, HEAD_SIZE), cosine_rows, sine_table
        )
        .reshape(token_rows, key_value_width)
        .astype(jnp.bfloat16)
    )
    value_pre_grad = value_local.astype(jnp.bfloat16)
    query_weight_grad = jnp.dot(normed_one.T, query_pre_grad, preferred_element_type=jnp.float32)
    key_weight_grad = jnp.dot(normed_one.T, key_pre_grad, preferred_element_type=jnp.float32)
    value_weight_grad = jnp.dot(normed_one.T, value_pre_grad, preferred_element_type=jnp.float32)
    normed_one_grad = (
        jnp.dot(query_pre_grad, whole_query.T, preferred_element_type=jnp.float32)
        + jnp.dot(key_pre_grad, whole_key.T, preferred_element_type=jnp.float32)
        + jnp.dot(value_pre_grad, whole_value.T, preferred_element_type=jnp.float32)
    )
    gain_one_grad, input_back = norm_backward(inputs_f, inverse_one, gain_one, normed_one_grad)
    input_grad = residual_grad + input_back
    (
        gain_one_sum,
        gain_two_sum,
        query_sum_all,
        key_sum_all,
        value_sum_all,
        output_sum_all,
        router_sum_all,
    ) = (
        lax.psum(gain_one_grad.astype(jnp.bfloat16), "ctx").astype(jnp.float32),
        lax.psum(gain_two_grad.astype(jnp.bfloat16), "ctx").astype(jnp.float32),
        lax.psum(query_weight_grad.astype(jnp.bfloat16), "ctx").astype(jnp.float32),
        lax.psum(key_weight_grad.astype(jnp.bfloat16), "ctx").astype(jnp.float32),
        lax.psum(value_weight_grad.astype(jnp.bfloat16), "ctx").astype(jnp.float32),
        lax.psum(output_grad.astype(jnp.bfloat16), "ctx").astype(jnp.float32),
        lax.psum(router_grad.astype(jnp.bfloat16), "ctx").astype(jnp.float32),
    )
    (
        gain_one_out,
        gain_two_out,
        query_out,
        key_out,
        value_out,
        output_out,
        router_out,
        inner_out,
        outer_out,
    ) = (
        lax.psum_scatter(
            gain_one_sum.astype(jnp.bfloat16), "wsh", scatter_dimension=0, tiled=True
        ).astype(jnp.float32),
        lax.psum_scatter(
            gain_two_sum.astype(jnp.bfloat16), "wsh", scatter_dimension=0, tiled=True
        ).astype(jnp.float32),
        lax.psum_scatter(
            query_sum_all.astype(jnp.bfloat16), "wsh", scatter_dimension=0, tiled=True
        ).astype(jnp.float32),
        lax.psum_scatter(
            key_sum_all.astype(jnp.bfloat16), "wsh", scatter_dimension=0, tiled=True
        ).astype(jnp.float32),
        lax.psum_scatter(
            value_sum_all.astype(jnp.bfloat16), "wsh", scatter_dimension=0, tiled=True
        ).astype(jnp.float32),
        lax.psum_scatter(
            output_sum_all.astype(jnp.bfloat16), "wsh", scatter_dimension=0, tiled=True
        ).astype(jnp.float32),
        lax.psum_scatter(
            router_sum_all.astype(jnp.bfloat16), "wsh", scatter_dimension=0, tiled=True
        ).astype(jnp.float32),
        lax.psum_scatter(
            inner_grad.astype(jnp.bfloat16), "wsh", scatter_dimension=1, tiled=True
        ).astype(jnp.float32),
        lax.psum_scatter(
            outer_grad.astype(jnp.bfloat16), "wsh", scatter_dimension=1, tiled=True
        ).astype(jnp.float32),
    )
    return (
        layer_output[None],
        input_grad[None],
        gain_one_out,
        query_out,
        key_out,
        value_out,
        output_out,
        gain_two_out,
        router_out,
        inner_out,
        outer_out,
    )


def solution(mesh):
    placed = (
        P("wsh", "ctx", None),
        P("wsh"),
        P("wsh", None),
        P("wsh", None),
        P("wsh", None),
        P("wsh", None),
        P("wsh"),
        P("wsh", None),
        P("ctx", "wsh", None),
        P("ctx", "wsh", None),
        P("wsh", None),
        P("wsh", None),
        P("wsh", "ctx", None),
        P("wsh", "ctx", None),
    )
    return jax.shard_map(
        on_device,
        mesh=mesh,
        in_specs=placed,
        out_specs=(
            P("wsh", "ctx", None),
            P("wsh", "ctx", None),
            P("wsh"),
            P("wsh", None),
            P("wsh", None),
            P("wsh", None),
            P("wsh", None),
            P("wsh"),
            P("wsh", None),
            P("ctx", "wsh", None),
            P("ctx", "wsh", None),
        ),
        check_vma=False,
    )
```

profile of v0, /device:TPU:0, one launch (start us, length us, event | category | flops | bytes accessed | tf_op | source)
XLA Modules:
  0.0 1914.6 jit_solution(13425614142795604898)
XLA Ops:
  35.4 17.8 all-gather.17.cloned.1.call-done
  71.4 33.8 %all-gather.13.cloned.1.call-done = bf16[2048,512]{1,0:T(8,128)(2,1)} async-done(((bf16[256,512]{1,0:T(8,128)(2,1)}), bf16[2048,512]{1,0:T(8,128)(2,1)}) %all-gather.13.cloned.1.call-update) | async-done | bytes 2097168 | tf_op jit(solution)/shard_map/all_gather | solution.py:152
  109.3 46.1 %all-gather.19.cloned.1.call-done = bf16[2048,512]{1,0:T(8,128)(2,1)} async-done(((bf16[256,512]{1,0:T(8,128)(2,1)}), bf16[2048,512]{1,0:T(8,128)(2,1)}) %all-gather.19.cloned.1.call-update) | async-done | bytes 2097168 | tf_op jit(solution)/shard_map/all_gather | solution.py:153
  159.5 33.3 %all-gather.15.cloned.1.call-done = bf16[1536,1536]{1,0:T(8,128)(2,1)} async-done(((bf16[384,1536]{1,0:T(8,128)(2,1)}), bf16[1536,1536]{1,0:T(8,128)(2,1)}) %all-gather.15.cloned.1.call-update) | async-done | bytes 4718608 | tf_op jit(solution)/shard_map/all_gather | solution.py:117
  204.2 89.0 %while.30 = (s32[]{:T(128)}, f32[8,3,256]{2,1,0:T(4,128)S(1)}, f32[8,3,256]{2,1,0:T(4,128)S(1)}, f32[8,3,256,64]{2,3,1,0:T(8,128)}, s32[256]{0:T(256)S(1)}, /*in...) while((s32[]{:T(128)}, f32[8,3,256]{2,1,0:T(4,128)S(1)}, ...), condition=%wide.region_7.8_spmd.clone, body=%wide.region_4.7_spmd.clone.sunk | while | flops 848197888 | bytes 96091824 | solution.py:198
  344.5 183.5 %all-to-all-done = bf16[8,2,192,1536]{3,2,1,0:T(8,128)(2,1)} async-done(((bf16[8,2,192,1536]{3,2,1,0:T(8,128)(2,1)}), bf16[8,2,192,1536]{3,2,1,0:T(8,128)(2,1)}, u32[]{:S(2)}, u32[]{:S(2)}) %all-to-all-start) | async-done | bytes 9437216 | tf_op jit(solution)/shard_map/all_to_all | solution.py:226
  534.6 47.6 %all-gather.23.cloned.1.call-done = bf16[2,1536,1024]{2,1,0:T(8,128)(2,1)} async-done(((bf16[2,384,1024]{2,1,0:T(8,128)(2,1)}), bf16[2,1536,1024]{2,1,0:T(8,128)(2,1)}) %all-gather.23.cloned.1.call-update) | async-done | bytes 6291472 | tf_op jit(solution)/shard_map/all_gather | solution.py:122
  582.3 17.0 fusion.49
  612.4 125.9 %all-to-all-done.2 = bf16[8,2,192,1536]{3,2,1,0:T(8,128)(2,1)} async-done(((bf16[8,2,192,1536]{3,2,1,0:T(8,128)(2,1)}), bf16[8,2,192,1536]{3,2,1,0:T(8,128)(2,1)}, u32[]{:S(2)}, u32[]{:S(2)}) %all-to-all-start.2) | async-done | bytes 9437216 | tf_op jit(solution)/shard_map/all_to_all | solution.py:259
  800.8 179.9 %all-to-all-done.1 = bf16[8,2,192,1536]{3,2,1,0:T(8,128)(2,1)} async-done(((bf16[8,2,192,1536]{3,2,1,0:T(8,128)(2,1)}), bf16[8,2,192,1536]{3,2,1,0:T(8,128)(2,1)}, u32[]{:S(2)}, u32[]{:S(2)}) %all-to-all-start.1) | async-done | bytes 9437216 | tf_op jit(solution)/shard_map/all_to_all | solution.py:237
  986.6 18.2 gather_fusion
  1004.8 16.5 fusion.23
  1021.5 168.9 %all-to-all-done.3 = bf16[8,2,192,1536]{3,2,1,0:T(8,128)(2,1)} async-done(((bf16[8,2,192,1536]{3,2,1,0:T(8,128)(2,1)}), bf16[8,2,192,1536]{3,2,1,0:T(8,128)(2,1)}, u32[]{:S(2)}, u32[]{:S(2)}) %all-to-all-start.3) | async-done | bytes 9437216 | tf_op jit(solution)/shard_map/all_to_all | solution.py:280
  1190.4 18.4 gather_fusion.1
  1224.8 117.5 %while.31 = (s32[]{:T(128)}, f32[8,3,256,64]{2,3,1,0:T(8,128)}, bf16[4,512,512]{2,1,0:T(8,128)(2,1)}, bf16[4,512,512]{2,1,0:T(8,128)(2,1)}, s32[256]{0:T(256)S(1...) while((s32[]{:T(128)}, f32[8,3,256,64]{2,3,1,0:T(8,128)}, ...), condition=%wide.region_25.26_spmd.clone, body=%wide.region_24.25_spmd.clone.sunk | while | flops 2047213824 | bytes 154296688 | solution.py:355
  1343.0 66.5 %reduce-scatter.12.cloned.1.call-done = bf16[256,512]{1,0:T(8,128)(2,1)} async-done(((bf16[2048,512]{1,0:T(8,128)(2,1)}), bf16[256,512]{1,0:T(8,128)(2,1)}) %reduce-scatter.12.cloned.1.call-update) | async-done | bytes 262160 | tf_op jit(solution)/shard_map/reduce_scatter | solution.py:360
  1412.7 67.4 %reduce-scatter.14.cloned.1.call-done = bf16[256,512]{1,0:T(8,128)(2,1)} async-done(((bf16[2048,512]{1,0:T(8,128)(2,1)}), bf16[256,512]{1,0:T(8,128)(2,1)}) %reduce-scatter.14.cloned.1.call-update) | async-done | bytes 262160 | tf_op jit(solution)/shard_map/reduce_scatter | solution.py:363
  1523.5 17.8 reduce-scatter.24.cloned.1.call-done
  1541.3 50.5 %reduce-scatter.26.cloned.1.call-done = bf16[384,1536]{1,0:T(8,128)(2,1)} async-done(((bf16[1536,1536]{1,0:T(8,128)(2,1)}), bf16[384,1536]{1,0:T(8,128)(2,1)}) %reduce-scatter.26.cloned.1.call-update) | async-done | bytes 1179664 | tf_op jit(solution)/shard_map/reduce_scatter | solution.py:437
  1591.8 50.4 %reduce-scatter.20.cloned.1.call-done = bf16[384,1536]{1,0:T(8,128)(2,1)} async-done(((bf16[1536,1536]{1,0:T(8,128)(2,1)}), bf16[384,1536]{1,0:T(8,128)(2,1)}) %reduce-scatter.20.cloned.1.call-update) | async-done | bytes 1179664 | tf_op jit(solution)/shard_map/reduce_scatter | solution.py:428
  1643.5 39.0 %reduce-scatter.18.cloned.1.call-done = bf16[2,128,1536]{2,1,0:T(8,128)(2,1)} async-done(((bf16[2,512,1536]{2,1,0:T(8,128)(2,1)}), bf16[2,128,1536]{2,1,0:T(8,128)(2,1)}) %reduce-scatter.18.cloned.1.call-update) | async-done | bytes 786448 | tf_op jit(solution)/shard_map/reduce_scatter | solution.py:446
  1685.0 58.8 %reduce-scatter.16.cloned.1.call-done = bf16[2,384,1024]{2,1,0:T(8,128)(2,1)} async-done(((bf16[2,1536,1024]{2,1,0:T(8,128)(2,1)}), bf16[2,384,1024]{2,1,0:T(8,128)(2,1)}) %reduce-scatter.16.cloned.1.call-update) | async-done | bytes 1572880 | tf_op jit(solution)/shard_map/reduce_scatter | solution.py:443
  1778.7 39.3 %all-reduce.2 = (bf16[384]{0:T(512)(128)(2,1)S(1)}, bf16[384]{0:T(512)(128)(2,1)S(1)}, bf16[384,16]{0,1:T(8,128)(2,1)S(1)}) all-reduce(bf16[384]{0:T(512)(128)(2,1)S(1)} %dynamic-slice.2, bf16[384]{0:T(512)(128)(2,1)S(1)} %dynamic-slice.4, bf16[384,16]{0,1:T(8,128)(2,1)S(1)} %copy.154), channel_id=1, replica_groups=mesh['ctx'=8,'wsh'=4] {'ctx'}, use_global_device_ids=true, to_apply=%region_30.31 | all-reduce | flops 6912 | bytes 27648 | tf_op jit(solution)/shard_map/psum | solution.py:403
  1822.9 77.9 %all-reduce.7.cloned.1.call-done = (bf16[384,1536]{1,0:T(8,128)(2,1)}, bf16[384,512]{1,0:T(8,128)(2,1)}, bf16[384,512]{1,0:T(8,128)(2,1)}, bf16[384,1536]{1,0:T(8,128)(2,1)}) async-done(((bf16[384,1536]{1,0:T(8,128)(2,1)}, bf16[384,512]{1,0:T(8,128)(2,1)}, bf16[384,512]{1,0:T(8,128)(2,1)}, bf16[384,1536]{1,0:T(8,128)(2,1)}), (bf16[384,1536]{1,0:T(8,128)(2,1)}, bf16[384,512]{1,0:T(8,128)(2,1)}, ...) | async-done | bytes 3145744 | tf_op jit(solution)/shard_map/psum | solution.py:405
  (413 shorter events, 523.0 us)
Async XLA Ops:
  7.2 24.8 %all-gather.11.cloned.1.call-start = ((), (), s32[]{:S(2)}) async-start(), calls=%async_computation.13 | async-start | bytes 1966080 | tf_op jit(solution)/shard_map/all_gather | solution.py:118
  7.9 45.3 %all-gather.17.cloned.1.call-start = ((), (), s32[]{:S(2)}) async-start(), calls=%async_computation.16 | async-start | bytes 1966080 | tf_op jit(solution)/shard_map/all_gather | solution.py:119
  8.7 96.5 %all-gather.13.cloned.1.call-start = ((), (), s32[]{:S(2)}) async-start(), calls=%async_computation.14 | async-start | bytes 2359296 | tf_op jit(solution)/shard_map/all_gather | solution.py:152
  35.4 120.0 %all-gather.19.cloned.1.call-start = ((), (), s32[]{:S(2)}) async-start(), calls=%async_computation.17 | async-start | bytes 2359296 | tf_op jit(solution)/shard_map/all_gather | solution.py:153
  55.9 136.9 %all-gather.15.cloned.1.call-start = ((), (), s32[]{:S(2)}) async-start(), calls=%async_computation.15 | async-start | bytes 5898240 | tf_op jit(solution)/shard_map/all_gather | solution.py:117
  56.5 238.6 %all-gather.21.cloned.1.call-start = ((), (), s32[]{:S(2)}) async-start(), calls=%async_computation.18 | async-start | bytes 5898240 | tf_op jit(solution)/shard_map/all_gather | solution.py:120
  65.7 233.5 %copy-start.33 = (f32[1536]{0:T(1024)}, f32[1536]{0:T(1024)S(1)}, u32[]{:S(2)}) copy-start(f32[1536]{0:T(1024)S(1)} %reshape.515) | copy-start | bytes 18436
  316.4 211.7 %all-to-all-start = ((bf16[8,2,192,1536]{3,2,1,0:T(8,128)(2,1)}), bf16[8,2,192,1536]{3,2,1,0:T(8,128)(2,1)}, u32[]{:S(2)}, u32[]{:S(2)}) async-start(bf16[8,2,192,1536]{3,2,1,0:T(8,128)(2,1)} %bitcast.333), calls=%async_computation | async-start | bytes 18874368 | tf_op jit(solution)/shard_map/all_to_all | solution.py:226
  528.0 210.2 %all-to-all-start.2 = ((bf16[8,2,192,1536]{3,2,1,0:T(8,128)(2,1)}), bf16[8,2,192,1536]{3,2,1,0:T(8,128)(2,1)}, u32[]{:S(2)}, u32[]{:S(2)}) async-start(bf16[8,2,192,1536]{3,2,1,0:T(8,128)(2,1)} %bitcast.332), calls=%async_computation.2 | async-start | bytes 18874368 | tf_op jit(solution)/shard_map/all_to_all | solution.py:259
  533.1 49.2 %all-gather.23.cloned.1.call-start = ((), (), s32[]{:S(2)}) async-start(), calls=%async_computation.19 | async-start | bytes 7864320 | tf_op jit(solution)/shard_map/all_gather | solution.py:122
  533.9 78.5 %all-gather.25.cloned.1.call-start = ((), (), s32[]{:S(2)}) async-start(), calls=%async_computation.20 | async-start | bytes 3932160 | tf_op jit(solution)/shard_map/all_gather | solution.py:123
  770.8 209.8 %all-to-all-start.1 = ((bf16[8,2,192,1536]{3,2,1,0:T(8,128)(2,1)}), bf16[8,2,192,1536]{3,2,1,0:T(8,128)(2,1)}, u32[]{:S(2)}, u32[]{:S(2)}) async-start(bf16[8,2,192,1536]{3,2,1,0:T(8,128)(2,1)} %copy.126), calls=%async_computation.1 | async-start | bytes 18874368 | tf_op jit(solution)/shard_map/all_to_all | solution.py:237
  980.6 209.7 %all-to-all-start.3 = ((bf16[8,2,192,1536]{3,2,1,0:T(8,128)(2,1)}), bf16[8,2,192,1536]{3,2,1,0:T(8,128)(2,1)}, u32[]{:S(2)}, u32[]{:S(2)}) async-start(bf16[8,2,192,1536]{3,2,1,0:T(8,128)(2,1)} %copy.131), calls=%async_computation.3 | async-start | bytes 18874368 | tf_op jit(solution)/shard_map/all_to_all | solution.py:280
  985.7 423.8 %reduce-scatter.12.cloned.1.call-start = ((), (), s32[]{:S(2)}) async-start(), calls=%async_computation.21 | async-start | bytes 2359296 | tf_op jit(solution)/shard_map/reduce_scatter | solution.py:360
  1021.5 194.5 %copy-start.40 = (bf16[256,16]{0,1:T(8,128)(2,1)}, bf16[256,16]{0,1:T(8,128)(2,1)S(1)}, u32[]{:S(2)}) copy-start(bf16[256,16]{0,1:T(8,128)(2,1)S(1)} %select_reduce_fusion) | copy-start | bytes 24580
  1342.4 137.7 %reduce-scatter.14.cloned.1.call-start = ((), (), s32[]{:S(2)}) async-start(), calls=%async_computation.22 | async-start | bytes 2359296 | tf_op jit(solution)/shard_map/reduce_scatter | solution.py:363
  1343.0 180.6 %reduce-scatter.22.cloned.1.call-start = ((), (), s32[]{:S(2)}) async-start(), calls=%async_computation.26 | async-start | bytes 1966080 | tf_op jit(solution)/shard_map/reduce_scatter | solution.py:431
  1412.7 128.7 %reduce-scatter.24.cloned.1.call-start = ((), (), s32[]{:S(2)}) async-start(), calls=%async_computation.27 | async-start | bytes 1966080 | tf_op jit(solution)/shard_map/reduce_scatter | solution.py:434
  1482.9 108.9 %reduce-scatter.26.cloned.1.call-start = ((), (), s32[]{:S(2)}) async-start(), calls=%async_computation.28 | async-start | bytes 5898240 | tf_op jit(solution)/shard_map/reduce_scatter | solution.py:437
  1488.2 154.0 %reduce-scatter.20.cloned.1.call-start = ((), (), s32[]{:S(2)}) async-start(), calls=%async_computation.25 | async-start | bytes 5898240 | tf_op jit(solution)/shard_map/reduce_scatter | solution.py:428
  1493.7 188.8 %reduce-scatter.18.cloned.1.call-start = ((), (), s32[]{:S(2)}) async-start(), calls=%async_computation.24 | async-start | bytes 3932160 | tf_op jit(solution)/shard_map/reduce_scatter | solution.py:446
  1504.4 239.4 %reduce-scatter.16.cloned.1.call-start = ((), (), s32[]{:S(2)}) async-start(), calls=%async_computation.23 | async-start | bytes 7864320 | tf_op jit(solution)/shard_map/reduce_scatter | solution.py:443
  1520.9 246.6 %reduce-scatter.28.cloned.1.call-start = ((), (), s32[]{:S(2)}) async-start(), calls=%async_computation.29 | async-start | bytes 491520
  1523.2 377.5 %all-reduce.7.cloned.1.call-start = ((), (), s32[]{:S(2)}) async-start(), calls=%async_computation.30 | async-start | bytes 6291456 | tf_op jit(solution)/shard_map/psum | solution.py:405
  (75 other events, 1745.1 us)
Sparse Core Ops, SparseCore 0:
  9.6 22.3 all-gather.10
  33.5 19.6 all-gather.16
  55.9 49.2 all-gather.12
  107.8 47.6 all-gather.18
  156.8 35.9 all-gather.14
  194.2 37.4 all-gather.20
  535.5 46.7 all-gather.22
  583.8 28.4 all-gather.24
  1342.5 66.9 reduce-scatter.11
  1412.9 67.1 reduce-scatter.13
  1483.2 27.0 reduce-scatter.21
  1513.3 27.9 reduce-scatter.23
  1543.9 47.9 reduce-scatter.25
  1594.2 47.9 reduce-scatter.19
  1644.6 37.8 reduce-scatter.17
  1684.9 58.8 reduce-scatter.15
  1746.7 20.8 reduce-scatter.27
  1771.3 129.4 all-reduce.6
where the time goes:
time: 1920 us; the launch traced here: 1910 us
  waiting for transfers between devices  1310 us (68%)
  matrix products  261 us (14%)
  local copies, waits for them, and re-layouts  138 us (7%)
  other arithmetic  103 us (5%)
  blocking collectives  62.3 us (3%)
  starting transfers between devices  22.5 us (1%)
    all_to_all x1, waiting for transfers between devices, on_device(): lax.all_to_all(send_rows, 'ctx', split_axis=0, concat_axis=0, tiled=True)  184 us
    all_to_all x1, waiting for transfers between devices, on_device(): lax.all_to_all(expert_result, 'ctx', split_axis=0, concat_axis=0, tiled=T...  180 us
    all_to_all x1, waiting for transfers between devices, on_device(): lax.all_to_all(row_grads, 'ctx', split_axis=0, concat_axis=0, tiled=True)  169 us
    all_to_all x1, waiting for transfers between devices, on_device(): lax.all_to_all(send_grads, 'ctx', split_axis=0, concat_axis=0, tiled=True)  126 us
    psum x1, waiting for transfers between devices, on_device(): lax.psum(query_weight_grad.astype(jnp.bfloat16), 'ctx').astype(jnp.float32)  77.9 us
    reduce_scatter x1, waiting for transfers between devices, on_device(): lax.psum_scatter(value_grad.astype(jnp.bfloat16), 'ctx', scatter_dimensio...  67.4 us
    reduce_scatter x1, waiting for transfers between devices, on_device(): lax.psum_scatter(key_grad.astype(jnp.bfloat16), 'ctx', scatter_dimension=...  66.5 us
    reduce_scatter x1, waiting for transfers between devices, on_device(): lax.psum_scatter(inner_grad.astype(jnp.bfloat16), 'wsh', scatter_dimensio...  58.8 us
  transfers between devices with their start and end apart: 22, of which 20 were waited for; matrix products, arithmetic and copies ran while one was open for 15% of the time, Pallas kernels for 0%

commit v1 on v0

v1 whole, which is shorter than its diff:
```python
import functools

import jax
import jax.numpy as jnp
from jax import lax
from jax.experimental import pallas as pl
from jax.experimental.pallas import tpu as pltpu
from jax.sharding import PartitionSpec as P

QUERY_HEADS = 24
KEY_HEADS = 8
HEAD_SIZE = 64
EXPERT_H = 512
TOPK = 8
SEQS = 4
GROUP = QUERY_HEADS // KEY_HEADS
PAIRS = KEY_HEADS // 2
PAIR_HEADS = 2 * GROUP
PAIR_WIDTH = 2 * HEAD_SIZE

EPS = 1e-05
THETA = 10000.0
MASK_FILL = -1e30
SCALE = HEAD_SIZE**-0.5
BF16 = jnp.bfloat16
F32 = jnp.float32


def dot(a, b):
    return jnp.dot(a, b, preferred_element_type=F32)


def dot_nt(a, b):
    return lax.dot_general(a, b, (((1,), (1,)), ((), ())), preferred_element_type=F32)


def dot_tn(a, b):
    return lax.dot_general(a, b, (((0,), (0,)), ((), ())), preferred_element_type=F32)


def rms_inverse(matrix):
    return lax.rsqrt(jnp.mean(matrix * matrix, axis=-1, keepdims=True) + EPS)


def locate(lengths_row, places_row):
    segment_ends = jnp.cumsum(lengths_row)
    beyond = (places_row[:, None] >= segment_ends[None, :]).astype(jnp.int32)
    documents = jnp.sum(beyond, axis=1)
    offsets = places_row - jnp.sum(beyond * lengths_row[None, :], axis=1)
    return (documents, offsets)


def angles_for(offsets):
    halfway = HEAD_SIZE // 2
    frequency = THETA ** (-2.0 * jnp.arange(halfway, dtype=F32) / HEAD_SIZE)
    angles = offsets.astype(F32)[:, None] * frequency[None, :]
    return (jnp.cos(angles)[:, None, :], jnp.sin(angles)[:, None, :])


def apply_rotation(matrix, cosine_rows, sine_table):
    halfway = matrix.shape[-1] // 2
    former = matrix[..., :halfway]
    latter = matrix[..., halfway:]
    return jnp.concatenate(
        [former * cosine_rows - latter * sine_table, latter * cosine_rows + former * sine_table],
        axis=-1,
    )


def reverse_rotation(matrix, cosine_rows, sine_table):
    return apply_rotation(matrix, cosine_rows, -sine_table)


def norm_backward(matrix, inverse, gains, gradients):
    scaled = gradients * gains
    gain_grad = jnp.sum(gradients * matrix * inverse, axis=0)
    input_back = inverse * scaled - matrix * inverse * inverse * inverse * jnp.mean(
        scaled * matrix, axis=-1, keepdims=True
    )
    return (gain_grad, input_back)


def spread_heads(rows):
    tokens = rows.shape[0]
    heads = rows.reshape(tokens, PAIRS, 2, GROUP, HEAD_SIZE).transpose(1, 2, 3, 4, 0)
    zero = jnp.zeros_like(heads[:, 0])
    low = jnp.concatenate([heads[:, 0], zero], axis=2)
    high = jnp.concatenate([zero, heads[:, 1]], axis=2)
    return jnp.stack([low, high], axis=1).reshape(PAIRS, PAIR_HEADS, PAIR_WIDTH, tokens)


def gather_heads(spread):
    tokens = spread.shape[-1]
    split = spread.reshape(PAIRS, 2, GROUP, 2, HEAD_SIZE, tokens)
    heads = jnp.stack([split[:, 0, :, 0], split[:, 1, :, 1]], axis=1)
    return heads.transpose(4, 0, 1, 2, 3).reshape(tokens, QUERY_HEADS * HEAD_SIZE)


def fill_bias(bias_ref, kdoc_ref, kplace_ref, qdoc_ref, qplace_ref):
    kdoc, kplace = kdoc_ref[...], kplace_ref[...]
    qdoc, qplace = qdoc_ref[...], qplace_ref[...]
    seen = (kdoc == qdoc) & (qdoc < SEQS) & (kplace <= qplace) | (kplace == qplace)
    bias_ref[...] = jnp.where(seen, 0.0, MASK_FILL)


def attend_kernel(
    q_ref, k_ref, v_ref, kdoc_ref, kplace_ref, qdoc_ref, qplace_ref, o_ref, lse_ref, bias, vt
):
    pair, head = pl.program_id(0), pl.program_id(1)

    @pl.when((pair == 0) & (head == 0))
    def _():
        fill_bias(bias, kdoc_ref, kplace_ref, qdoc_ref, qplace_ref)

    @pl.when(head == 0)
    def _():
        vt[...] = v_ref[...].T

    scores = dot(k_ref[...], q_ref[0, 0]) + bias[...]
    top = jnp.max(scores, axis=0, keepdims=True)
    weights = jnp.exp(scores - top)
    total = jnp.sum(weights, axis=0, keepdims=True)
    o_ref[0, 0] = dot(vt[...], weights.astype(BF16)) / total
    lse_ref[0, 0] = top + jnp.log(total)


def attend_back_kernel(
    q_ref,
    qt_ref,
    g_ref,
    gt_ref,
    k_ref,
    v_ref,
    lse_ref,
    delta_ref,
    kdoc_ref,
    kplace_ref,
    qdoc_ref,
    qplace_ref,
    dq_ref,
    dk_ref,
    dv_ref,
    bias,
    kt,
    dk_sum,
    dv_sum,
):
    pair, head = pl.program_id(0), pl.program_id(1)

    @pl.when((pair == 0) & (head == 0))
    def _():
        fill_bias(bias, kdoc_ref, kplace_ref, qdoc_ref, qplace_ref)

    @pl.when(head == 0)
    def _():
        kt[...] = k_ref[...].T
        dk_sum[...] = jnp.zeros_like(dk_sum)
        dv_sum[...] = jnp.zeros_like(dv_sum)

    scores = dot(k_ref[...], q_ref[0, 0]) + bias[...]
    probs = jnp.exp(scores - lse_ref[0, 0])
    prob_grad = dot(v_ref[...], g_ref[0, 0])
    score_grad = (probs * (prob_grad - delta_ref[0, 0])).astype(BF16)
    dv_sum[...] += dot(probs.astype(BF16), gt_ref[0, 0])
    dk_sum[...] += dot(score_grad, qt_ref[0, 0])
    dq_ref[0, 0] = dot(kt[...], score_grad)

    @pl.when(head == PAIR_HEADS - 1)
    def _():
        dk_ref[...] = dk_sum[...].astype(BF16)
        dv_ref[...] = dv_sum[...].astype(BF16)


def whole(shape):
    return pl.BlockSpec(shape, lambda *_: (0,) * len(shape))


def attention_specs(tokens, rows):
    head = pl.BlockSpec((1, 1, PAIR_WIDTH, tokens), lambda p, h: (p, h, 0, 0))
    head_t = pl.BlockSpec((1, 1, tokens, PAIR_WIDTH), lambda p, h: (p, h, 0, 0))
    line = pl.BlockSpec((1, 1, 1, tokens), lambda p, h: (p, h, 0, 0))
    keys = pl.BlockSpec((rows, PAIR_WIDTH), lambda p, h: (0, p))
    marks = [whole((rows, 1)), whole((rows, 1)), whole((1, tokens)), whole((1, tokens))]
    return head, head_t, line, keys, marks


def attend(queries, keys, values, marks):
    tokens, rows = queries.shape[-1], keys.shape[0]
    head, _, line, key_spec, mark_specs = attention_specs(tokens, rows)
    return pl.pallas_call(
        attend_kernel,
        grid=(PAIRS, PAIR_HEADS),
        in_specs=[head, key_spec, key_spec] + mark_specs,
        out_specs=[head, line],
        out_shape=[
            jax.ShapeDtypeStruct((PAIRS, PAIR_HEADS, PAIR_WIDTH, tokens), F32),
            jax.ShapeDtypeStruct((PAIRS, PAIR_HEADS, 1, tokens), F32),
        ],
        scratch_shapes=[pltpu.VMEM((rows, tokens), F32), pltpu.VMEM((PAIR_WIDTH, rows), BF16)],
        cost_estimate=pl.CostEstimate(
            flops=4 * QUERY_HEADS * tokens * rows * PAIR_WIDTH,
            bytes_accessed=16 << 20,
            transcendentals=QUERY_HEADS * tokens * rows,
        ),
        name="attend",
    )(queries, keys, values, *marks)


def attend_back(queries, queries_t, grads, grads_t, keys, values, lse, delta, marks):
    tokens, rows = queries.shape[-1], keys.shape[0]
    head, head_t, line, key_spec, mark_specs = attention_specs(tokens, rows)
    return pl.pallas_call(
        attend_back_kernel,
        grid=(PAIRS, PAIR_HEADS),
        in_specs=[head, head_t, head, head_t, key_spec, key_spec, line, line] + mark_specs,
        out_specs=[head, key_spec, key_spec],
        out_shape=[
            jax.ShapeDtypeStruct((PAIRS, PAIR_HEADS, PAIR_WIDTH, tokens), F32),
            jax.ShapeDtypeStruct(keys.shape, BF16),
            jax.ShapeDtypeStruct(keys.shape, BF16),
        ],
        scratch_shapes=[
            pltpu.VMEM((rows, tokens), F32),
            pltpu.VMEM((PAIR_WIDTH, rows), BF16),
            pltpu.VMEM((rows, PAIR_WIDTH), F32),
            pltpu.VMEM((rows, PAIR_WIDTH), F32),
        ],
        cost_estimate=pl.CostEstimate(
            flops=10 * QUERY_HEADS * tokens * rows * PAIR_WIDTH,
            bytes_accessed=24 << 20,
            transcendentals=QUERY_HEADS * tokens * rows,
        ),
        name="attend_back",
    )(queries, queries_t, grads, grads_t, keys, values, lse, delta, *marks)


def expert_kernel(
    x_ref, g_ref, w_ref, wi_ref, wo_ref, mix_ref, back_ref, gate_ref, dwi_ref, dwo_ref, dwi, dwo, mid, rows
):
    step = pl.program_id(0)
    count, width = wi_ref.shape[0], wi_ref.shape[1]

    @pl.when(step == 0)
    def _():
        dwi[...] = jnp.zeros_like(dwi)
        dwo[...] = jnp.zeros_like(dwo)

    grad = g_ref[...]
    for e in range(count):
        gate_up = dot(x_ref[...], wi_ref[e])
        gate, up = gate_up[:, :EXPERT_H], gate_up[:, EXPERT_H:]
        sigmoid = 1.0 / (1.0 + jnp.exp(-gate))
        silu = gate * sigmoid
        hidden = (silu * up).astype(BF16).astype(F32)
        weight = w_ref[:, e : e + 1]
        inward = dot_nt(grad, wo_ref[e])
        gate_ref[:, e : e + 1] = jnp.sum(hidden * inward, axis=1, keepdims=True)
        weighted = (weight * hidden).astype(BF16)
        hidden_grad = weight * inward
        mid[:, e * EXPERT_H : (e + 1) * EXPERT_H] = weighted
        at = 2 * e * EXPERT_H
        rows[:, at : at + EXPERT_H] = (
            hidden_grad * up * sigmoid * (1.0 + gate * (1.0 - sigmoid))
        ).astype(BF16)
        rows[:, at + EXPERT_H : at + 2 * EXPERT_H] = (hidden_grad * silu).astype(BF16)
        dwo[e] += dot_tn(weighted, grad)
    tile = 256
    for e in range(count):
        inner = rows[:, 2 * e * EXPERT_H : 2 * (e + 1) * EXPERT_H]

        @pl.loop(0, width // tile)
        def _(t):
            at = pl.multiple_of(t * tile, tile)
            dwi[e, pl.ds(at, tile), :] += dot_tn(x_ref[:, pl.ds(at, tile)], inner)

    @pl.loop(0, width // tile)
    def _(t):
        at = pl.multiple_of(t * tile, tile)
        mixed, back = 0.0, 0.0
        for e in range(count):
            mixed += dot(mid[:, e * EXPERT_H : (e + 1) * EXPERT_H], wo_ref[e, :, pl.ds(at, tile)])
            back += dot_nt(
                rows[:, 2 * e * EXPERT_H : 2 * (e + 1) * EXPERT_H], wi_ref[e, pl.ds(at, tile), :]
            )
        mix_ref[:, pl.ds(at, tile)] = mixed.astype(BF16)
        back_ref[:, pl.ds(at, tile)] = back.astype(BF16)

    @pl.when(step == pl.num_programs(0) - 1)
    def _():
        dwi_ref[...] = dwi[...].astype(BF16)
        dwo_ref[...] = dwo[...].astype(BF16)


def experts_pass(tokens, grads, weights, inner, outer):
    rows, width = tokens.shape
    block = 256
    row_spec = pl.BlockSpec((block, width), lambda i: (i, 0))
    count = inner.shape[0]
    gate_spec = pl.BlockSpec((block, count), lambda i: (i, 0))
    once = pl.Buffered(1)
    inner_spec = pl.BlockSpec(inner.shape, lambda i: (0, 0, 0), pipeline_mode=once)
    outer_spec = pl.BlockSpec(outer.shape, lambda i: (0, 0, 0), pipeline_mode=once)
    return pl.pallas_call(
        expert_kernel,
        grid=(rows // block,),
        in_specs=[row_spec, row_spec, gate_spec, inner_spec, outer_spec],
        out_specs=[row_spec, row_spec, gate_spec, inner_spec, outer_spec],
        out_shape=[
            jax.ShapeDtypeStruct((rows, width), BF16),
            jax.ShapeDtypeStruct((rows, width), BF16),
            jax.ShapeDtypeStruct((rows, count), F32),
            jax.ShapeDtypeStruct(inner.shape, BF16),
            jax.ShapeDtypeStruct(outer.shape, BF16),
        ],
        scratch_shapes=[
            pltpu.VMEM(inner.shape, F32),
            pltpu.VMEM(outer.shape, F32),
            pltpu.VMEM((block, count * EXPERT_H), BF16),
            pltpu.VMEM((block, 2 * count * EXPERT_H), BF16),
        ],
        compiler_params=pltpu.CompilerParams(vmem_limit_bytes=60 << 20),
        cost_estimate=pl.CostEstimate(
            flops=18 * count * rows * width * EXPERT_H,
            bytes_accessed=48 << 20,
            transcendentals=rows * count * EXPERT_H,
        ),
        name="experts",
    )(tokens, grads, weights, inner, outer)


MESH = pl.DeviceIdType.MESH
SLOW = 4
CHUNKS = 2


def ring_position(index, size):
    fast = size // SLOW
    row, column = lax.div(index, fast), lax.rem(index, fast)
    back = SLOW - 1 - row
    odd = lax.rem(back, 2)
    along = (column - 1) * (1 - odd) + (fast - 1 - column) * odd
    away = lax.div(column + fast - 2, fast - 1)
    return (1 - away) * row + away * (SLOW + back * (fast - 1) + along)


def ring_index(position, size):
    fast = size // SLOW
    away = lax.div(lax.div(position, SLOW) + fast - 2, fast - 1)
    rest = away * (position - SLOW)
    back, step = lax.div(rest, fast - 1), lax.rem(rest, fast - 1)
    odd = lax.rem(back, 2)
    column = (1 + step) * (1 - odd) + (fast - 1 - step) * odd
    return (1 - away) * position * fast + away * ((SLOW - 1 - back) * fast + column)


class Ring:
    def __init__(self, size):
        self.size, self.steps = size, size // 2
        self.me = lax.axis_index("ctx")
        self.place = ring_position(self.me, size)

    def at(self, shift):
        return ring_index(lax.rem(self.place + shift + self.size, self.size), self.size)

    def toward(self, direction, distance):
        return self.at(distance if direction == 0 else -distance)

    def device(self, direction):
        return (self.toward(direction, 1), lax.axis_index("wsh"))

    def meet(self):
        barrier = pltpu.get_barrier_semaphore()
        for direction in range(2):
            pl.semaphore_signal(
                barrier, inc=1, device_id=self.device(direction), device_id_type=MESH
            )
        pl.semaphore_wait(barrier, 2)

    def chunks(self, direction, last):
        if not last:
            return range(CHUNKS)
        half = CHUNKS // 2
        return range(half) if direction == 0 else range(half, CHUNKS)


def rows_at(block, rows, chunk):
    part = rows // CHUNKS
    return pl.ds(pl.multiple_of(block * rows + chunk * part, part), part)


def ring_gather_kernel(size, count, *refs):
    locals_, outs = refs[:count], refs[count : 2 * count]
    send, recv, own = refs[2 * count :]
    ring = Ring(size)
    ring.meet()

    def copy(k, direction, step, chunk, block):
        rows = locals_[k].shape[0]
        source = (
            locals_[k].at[rows_at(0, rows, chunk)]
            if step == 0
            else outs[k].at[rows_at(block, rows, chunk)]
        )
        return pltpu.make_async_remote_copy(
            src_ref=source,
            dst_ref=outs[k].at[rows_at(block, rows, chunk)],
            send_sem=send.at[k, direction, step, chunk],
            recv_sem=recv.at[k, direction, step, chunk],
            device_id=ring.device(direction),
            device_id_type=MESH,
        )

    started = []
    kept = []
    for step in range(ring.steps):
        for chunk in range(CHUNKS):
            for direction in range(2):
                if step > 0:
                    for k in range(count):
                        block = ring.toward(1 - direction, step)
                        copy(k, direction, step - 1, chunk, block).wait_recv()
                if chunk in ring.chunks(direction, step == ring.steps - 1):
                    for k in range(count):
                        moved = copy(k, direction, step, chunk, ring.toward(1 - direction, step))
                        moved.start()
                        started.append(moved)
        if step == 0:
            for k in range(count):
                rows = locals_[k].shape[0]
                place = pl.ds(pl.multiple_of(ring.me * rows, rows), rows)
                kept.append(pltpu.make_async_copy(locals_[k], outs[k].at[place], own.at[k]))
                kept[-1].start()
    last = ring.steps - 1
    for direction in range(2):
        for chunk in ring.chunks(direction, True):
            for k in range(count):
                copy(k, direction, last, chunk, ring.toward(1 - direction, last + 1)).wait_recv()
    for moved in started:
        moved.wait_send()
    for moved in kept:
        moved.wait()


def ring_gather(arrays, size, identity, name):
    count = len(arrays)
    sems = pltpu.SemaphoreType.DMA((count, 2, size // 2, CHUNKS))
    return pl.pallas_call(
        functools.partial(ring_gather_kernel, size, count),
        in_specs=[pl.BlockSpec(memory_space=pltpu.VMEM)] * count,
        out_specs=[pl.BlockSpec(memory_space=pl.ANY)] * count,
        out_shape=[
            jax.ShapeDtypeStruct((size * a.shape[0],) + a.shape[1:], a.dtype) for a in arrays
        ],
        scratch_shapes=[sems, sems, pltpu.SemaphoreType.DMA((count,))],
        compiler_params=pltpu.CompilerParams(collective_id=identity, has_side_effects=True),
        cost_estimate=pl.CostEstimate(flops=0, bytes_accessed=100 << 20, transcendentals=0),
        name=name,
    )(*arrays)


def ring_scatter_kernel(size, count, *refs):
    parts, outs = refs[:count], refs[count : 2 * count]
    stages, lands = refs[2 * count : 3 * count], refs[3 * count : 4 * count]
    send, recv = refs[4 * count :]
    ring = Ring(size)
    ring.meet()

    def copy(k, direction, step, chunk):
        rows = outs[k].shape[0]
        if step == 0:
            source = parts[k].at[rows_at(ring.toward(direction, ring.steps), rows, chunk)]
        else:
            source = stages[k].at[direction, step - 1, rows_at(0, rows, chunk)]
        return pltpu.make_async_remote_copy(
            src_ref=source,
            dst_ref=lands[k].at[direction, step, rows_at(0, rows, chunk)],
            send_sem=send.at[k, direction, step, chunk],
            recv_sem=recv.at[k, direction, step, chunk],
            device_id=ring.device(direction),
            device_id_type=MESH,
        )

    started = []
    for step in range(ring.steps):
        for chunk in range(CHUNKS):
            for direction in range(2):
                for k in range(count):
                    rows = outs[k].shape[0]
                    if step == 0:
                        if chunk not in ring.chunks(direction, True):
                            continue
                    else:
                        here = rows_at(0, rows, chunk)
                        dest = ring.toward(direction, ring.steps - step)
                        total = parts[k][rows_at(dest, rows, chunk)]
                        if step > 1 or chunk in ring.chunks(direction, True):
                            copy(k, direction, step - 1, chunk).wait_recv()
                            landed = lands[k][direction, step - 1, here]
                            total = (total.astype(F32) + landed.astype(F32)).astype(total.dtype)
                        stages[k][direction, step - 1, here] = total
                    moved = copy(k, direction, step, chunk)
                    moved.start()
                    started.append(moved)
    last = ring.steps - 1
    for chunk in range(CHUNKS):
        for k in range(count):
            rows = outs[k].shape[0]
            here = rows_at(0, rows, chunk)
            total = parts[k][rows_at(ring.me, rows, chunk)].astype(F32)
            for direction in range(2):
                copy(k, direction, last, chunk).wait_recv()
                total += lands[k][direction, last, here].astype(F32)
            outs[k][here] = total
    for moved in started:
        moved.wait_send()


def ring_scatter(arrays, size, identity, name):
    count, steps = len(arrays), size // 2
    sems = pltpu.SemaphoreType.DMA((count, 2, steps, CHUNKS))
    blocks = [(a.shape[0] // size,) + a.shape[1:] for a in arrays]
    vmem = pl.BlockSpec(memory_space=pltpu.VMEM)
    return pl.pallas_call(
        functools.partial(ring_scatter_kernel, size, count),
        in_specs=[vmem] * count,
        out_specs=[vmem] * count,
        out_shape=[jax.ShapeDtypeStruct(b, F32) for b in blocks],
        scratch_shapes=[
            pltpu.VMEM((2, steps - 1) + b, a.dtype) for a, b in zip(arrays, blocks)
        ]
        + [pltpu.VMEM((2, steps) + b, a.dtype) for a, b in zip(arrays, blocks)]
        + [sems, sems],
        compiler_params=pltpu.CompilerParams(
            collective_id=identity, has_side_effects=True, vmem_limit_bytes=48 << 20
        ),
        cost_estimate=pl.CostEstimate(flops=0, bytes_accessed=100 << 20, transcendentals=0),
        name=name,
    )(*arrays)


def on_device(
    layer_input,
    attention_gain,
    query_weight,
    key_matrix,
    value_matrix,
    output_weight,
    expert_gain,
    router_weight,
    expert_inner,
    expert_outer,
    document_lengths,
    token_places,
    expert_routes,
    cotangent,
):
    group_devices = lax.axis_size("ctx")
    ctx_index = lax.axis_index("ctx")
    token_rows = layer_input.shape[1]
    experts = router_weight.shape[1]
    own_experts = expert_inner.shape[0]
    key_value_width = KEY_HEADS * HEAD_SIZE

    def gather(shard, axis=0):
        return lax.all_gather(shard, "wsh", axis=axis, tiled=True)

    small = gather(
        jnp.concatenate([attention_gain[:, None], expert_gain[:, None], router_weight], axis=1)
    )
    gain_one, gain_two = small[:, 0].astype(F32), small[:, 1].astype(F32)
    whole_router = small[:, 2:]
    whole_key = gather(key_matrix)
    whole_value = gather(value_matrix)
    whole_query = gather(query_weight)
    whole_output = gather(output_weight)
    whole_inner = gather(expert_inner, 1)
    whole_outer = gather(expert_outer, 1)
    all_grads = lax.all_gather(cotangent[0], "ctx", axis=0, tiled=True)

    places_all = token_places[0]
    key_documents, key_offsets = locate(document_lengths[0], places_all)
    first_row = ctx_index * token_rows
    query_places = lax.dynamic_slice_in_dim(places_all, first_row, token_rows)
    query_documents = lax.dynamic_slice_in_dim(key_documents, first_row, token_rows)
    query_offsets = lax.dynamic_slice_in_dim(key_offsets, first_row, token_rows)
    marks = (
        key_documents[:, None],
        places_all[:, None],
        query_documents[None, :],
        query_places[None, :],
    )
    cosine_rows, sine_table = angles_for(query_offsets)

    inputs_f = layer_input[0].astype(F32)
    inverse_one = rms_inverse(inputs_f)
    normed_one = (inputs_f * inverse_one * gain_one).astype(BF16)
    key_pre = dot(normed_one, whole_key)
    keys = (
        apply_rotation(key_pre.reshape(token_rows, KEY_HEADS, HEAD_SIZE), cosine_rows, sine_table)
        .astype(BF16)
        .reshape(token_rows, key_value_width)
    )
    values = dot(normed_one, whole_value).astype(BF16)
    all_keys, all_values = ring_gather([keys, values], group_devices, 1, "gather_keys")
    query_pre = dot(normed_one, whole_query)
    queries = (
        apply_rotation(
            query_pre.reshape(token_rows, QUERY_HEADS, HEAD_SIZE), cosine_rows, sine_table
        ).astype(BF16)
        * SCALE
    ).reshape(token_rows, QUERY_HEADS * HEAD_SIZE)
    spread_queries = spread_heads(queries)
    spread_attended, lse = attend(spread_queries, all_keys, all_values, marks)
    attended_f = gather_heads(spread_attended)
    attended = attended_f.astype(BF16)
    residual = inputs_f + dot(attended, whole_output)
    inverse_two = rms_inverse(residual)
    normed_two = (residual * inverse_two * gain_two).astype(BF16)
    logits = dot(normed_two, whole_router)
    expert_ids = jnp.arange(experts, dtype=jnp.int32)
    routed = jnp.any(expert_routes[0][:, :, None] == expert_ids[None, None, :], axis=1)
    gates = jax.nn.softmax(jnp.where(routed, logits, -jnp.inf), axis=-1)

    all_tokens, all_gates = ring_gather([normed_two, gates.T], group_devices, 2, "gather_tokens")
    own_gates = (
        lax.dynamic_slice_in_dim(
            all_gates.reshape(group_devices, experts, token_rows),
            ctx_index * own_experts,
            own_experts,
            axis=1,
        )
        .transpose(0, 2, 1)
        .reshape(group_devices * token_rows, own_experts)
    )
    mixed, back_rows, own_gate_grad, inner_grad, outer_grad = experts_pass(
        all_tokens, all_grads, own_gates, whole_inner, whole_outer
    )
    placed = lax.dynamic_update_slice_in_dim(
        jnp.zeros((group_devices, experts, token_rows), F32),
        own_gate_grad.reshape(group_devices, token_rows, own_experts).transpose(0, 2, 1),
        ctx_index * own_experts,
        axis=1,
    ).reshape(group_devices * experts, token_rows)
    back_sum, gate_grad = ring_scatter([back_rows, placed], group_devices, 3, "scatter_rows")
    gate_grad = gate_grad.T
    mixture = lax.psum_scatter(mixed, "ctx", scatter_dimension=0, tiled=True)
    layer_output = (residual + mixture.astype(F32)).astype(BF16)

    out_grad = cotangent[0].astype(F32)
    logit_grad = (
        gates * (gate_grad - jnp.sum(gates * gate_grad, axis=-1, keepdims=True))
    ).astype(BF16)
    router_grad = dot_tn(normed_two, logit_grad)
    normed_two_grad = dot_nt(logit_grad, whole_router) + back_sum
    gain_two_grad, residual_back = norm_backward(residual, inverse_two, gain_two, normed_two_grad)
    residual_grad = out_grad + residual_back
    branch_grad = residual_grad.astype(BF16)
    output_grad = dot_tn(attended, branch_grad)
    attended_grad = dot_nt(branch_grad, whole_output).astype(BF16)
    delta = jnp.sum(
        (attended_grad.astype(F32) * attended_f).reshape(token_rows, QUERY_HEADS, HEAD_SIZE), axis=-1
    ).T.reshape(PAIRS, PAIR_HEADS, 1, token_rows)
    spread_grads = spread_heads(attended_grad)
    spread_query_grad, key_part, value_part = attend_back(
        spread_queries,
        spread_queries.transpose(0, 1, 3, 2),
        spread_grads,
        spread_grads.transpose(0, 1, 3, 2),
        all_keys,
        all_values,
        lse,
        delta,
        marks,
    )
    key_grad, value_grad = ring_scatter([key_part, value_part], group_devices, 4, "scatter_keys")
    value_grad = value_grad.astype(BF16)
    query_pre_grad = (
        reverse_rotation(
            (gather_heads(spread_query_grad) * SCALE).reshape(token_rows, QUERY_HEADS, HEAD_SIZE),
            cosine_rows,
            sine_table,
        )
        .reshape(token_rows, QUERY_HEADS * HEAD_SIZE)
        .astype(BF16)
    )
    key_pre_grad = (
        reverse_rotation(
            key_grad.reshape(token_rows, KEY_HEADS, HEAD_SIZE), cosine_rows, sine_table
        )
        .reshape(token_rows, key_value_width)
        .astype(BF16)
    )
    query_weight_grad = dot_tn(normed_one, query_pre_grad)
    key_weight_grad = dot_tn(normed_one, key_pre_grad)
    value_weight_grad = dot_tn(normed_one, value_grad)
    normed_one_grad = (
        dot_nt(query_pre_grad, whole_query)
        + dot_nt(key_pre_grad, whole_key)
        + dot_nt(value_grad, whole_value)
    )
    gain_one_grad, input_back = norm_backward(inputs_f, inverse_one, gain_one, normed_one_grad)
    input_grad = residual_grad + input_back

    def scatter(grad, dim=0):
        return lax.psum_scatter(grad.astype(BF16), "wsh", scatter_dimension=dim, tiled=True)

    def reduce(grad):
        return lax.psum(scatter(grad), "ctx").astype(F32)

    inner_out = scatter(inner_grad, 1).astype(F32)
    outer_out = scatter(outer_grad, 1).astype(F32)
    output_out = reduce(output_grad)
    query_out = reduce(query_weight_grad)
    key_value_out = reduce(jnp.concatenate([key_weight_grad, value_weight_grad], axis=1))
    small_out = reduce(
        jnp.concatenate([gain_one_grad[:, None], gain_two_grad[:, None], router_grad], axis=1)
    )
    return (
        layer_output[None],
        input_grad[None],
        small_out[:, 0],
        query_out,
        key_value_out[:, :key_value_width],
        key_value_out[:, key_value_width:],
        output_out,
        small_out[:, 1],
        small_out[:, 2:],
        inner_out,
        outer_out,
    )


def solution(mesh):
    tokens = P("wsh", "ctx", None)
    shard, expert = P("wsh", None), P("ctx", "wsh", None)
    return jax.shard_map(
        on_device,
        mesh=mesh,
        in_specs=(
            tokens,
            P("wsh"),
            shard,
            shard,
            shard,
            shard,
            P("wsh"),
            shard,
            expert,
            expert,
            shard,
            shard,
            tokens,
            tokens,
        ),
        out_specs=(
            tokens,
            tokens,
            P("wsh"),
            shard,
            shard,
            shard,
            shard,
            P("wsh"),
            shard,
            expert,
            expert,
        ),
        check_vma=False,
    )
```

time: 1920 us -> 1130 us (0.59)
  waiting for transfers between devices: 1310 us -> 468 us
  Pallas kernels: 0 us -> 465 us
  matrix products: 261 us -> 36.8 us
  local copies, waits for them, and re-layouts: 138 us -> 56.9 us
  other arithmetic: 103 us -> 27.3 us
  starting transfers between devices: 22.5 us -> 0.8 us
    all_to_all x4 -> x0, waiting for transfers between devices: 658 us -> none  [the longest x1 184 us: on_device(): lax.all_to_all(send_rows, 'ctx', split_axis=0, concat_axis=0, tiled=True)]
    pallas_call x0 -> x7, Pallas kernels: none -> 465 us  [the longest x2 159 us: ring_scatter(): pl.pallas_call(functools.partial(ring_scatter_kernel, size, count), in_sp...]
    dot_general x49 -> x15, matrix products: 261 us -> 36.8 us  [the longest x5 13.3 us: dot_nt(): lax.dot_general(a, b, (((1,), (1,)), ((), ())), preferred_element_type=F32)]
    all_gather x8 -> x7, waiting for transfers between devices: 204 us -> 92.1 us  [the longest x1 65.8 us: on_device(): all_grads = lax.all_gather(cotangent[0], 'ctx', axis=0, tiled=True)]
    reduce_scatter x8 -> x5, waiting for transfers between devices: 350 us -> 245 us  [the longest x4 198 us: scatter(): lax.psum_scatter(grad.astype(BF16), 'wsh', scatter_dimension=dim, tiled=T...]
    reduce_sum x13 -> x4, other arithmetic: 52.9 us -> 1.72 us  [the longest x1 1.55 us: on_device(): jnp.sum((attended_grad.astype(F32) * attended_f).reshape(token_rows, QUER...]
    gather x2 -> x0, local copies, waits for them, and re-layouts: 36.6 us -> none  [the longest x1 18.4 us: on_device(): back_rows.reshape(experts * capacity, model_width)[slot_index]]
    dynamic_slice x24 -> x1, local copies, waits for them, and re-layouts: 23.8 us -> 0.86 us  [on_device(): lax.dynamic_slice_in_dim(all_gates.reshape(group_devices, experts, token_...]
  transfers between devices with their start and end apart: 22 -> 15, of which waited for: 20 -> 11; matrix products, arithmetic and copies ran while one was open for 15% -> 7% of each run, Pallas kernels for 0% -> 25%
where the time goes in v1:
time: 1130 us; the launch traced here: 1120 us
  waiting for transfers between devices  468 us (41%)
  Pallas kernels  465 us (41%)
  local copies, waits for them, and re-layouts  56.9 us (5%)
  blocking collectives  45.5 us (4%)
  matrix products  36.8 us (3%)
  other arithmetic  27.3 us (2%)
  between operations  14.8 us (1%)
    reduce_scatter x4, waiting for transfers between devices, scatter(): lax.psum_scatter(grad.astype(BF16), 'wsh', scatter_dimension=dim, tiled=T...  198 us
    pallas_call x2, Pallas kernels, ring_scatter(): pl.pallas_call(functools.partial(ring_scatter_kernel, size, count), in_sp...  159 us
    pallas_call x2, Pallas kernels, ring_gather(): pl.pallas_call(functools.partial(ring_gather_kernel, size, count), in_spe...  129 us
    pallas_call x1, Pallas kernels, experts_pass(): pl.pallas_call(expert_kernel, grid=(rows // block,), in_specs=[row_spec,...  102 us
    psum x1, waiting for transfers between devices, reduce(): return lax.psum(scatter(grad), 'ctx').astype(F32)  92.3 us
    all_gather x1, waiting for transfers between devices, on_device(): all_grads = lax.all_gather(cotangent[0], 'ctx', axis=0, tiled=True)  65.8 us
    reduce_scatter x1, waiting for transfers between devices, on_device(): mixture = lax.psum_scatter(mixed, 'ctx', scatter_dimension=0, tiled=True)  46.4 us
    pallas_call x1, Pallas kernels, attend_back(): pl.pallas_call(attend_back_kernel, grid=(PAIRS, PAIR_HEADS), in_specs=[he...  41.3 us
  transfers between devices with their start and end apart: 15, of which 11 were waited for; matrix products, arithmetic and copies ran while one was open for 7% of the time, Pallas kernels for 25%

profile of v1, /device:TPU:0, one launch (start us, length us, event | category | flops | bytes accessed | tf_op | source)
XLA Modules:
  0.0 1115.4 jit_solution(6011001314181032784)
XLA Ops:
  15.7 6.3 all_gather.24
  23.8 8.2 all-gather.11.cloned.1.call-done
  35.3 18.1 %all-gather.13.cloned.1.call-done = bf16[1536,512]{1,0:T(8,128)(2,1)} async-done(((bf16[384,512]{1,0:T(8,128)(2,1)}), bf16[1536,512]{1,0:T(8,128)(2,1)}) %all-gather.13.cloned.1.call-update) | async-done | bytes 1572880 | tf_op jit(solution)/shard_map/all_gather | solution.py:565
  56.1 46.9 %gather_keys.1 = (bf16[2048,512]{1,0:T(8,128)(2,1)}, bf16[2048,512]{1,0:T(8,128)(2,1)}) custom-call(bf16[256,512]{1,0:T(8,128)(2,1)} %copy.108.refs_0_, bf16[256,512]{1,0:T(8,128)(2,1)} %convolution_convert_fusion.6.refs_1_), custom_call_target="tpu_custom_call" | custom-call | bytes 104857600 | tf_op jit(solution)/shard_map/gather_keys/pallas_call | solution.py:447
  103.0 6.7 copy.103
  121.0 34.4 %attend.1 = (f32[4,6,128,256]{3,2,1,0:T(8,128)}, f32[4,6,1,256]{3,2,1,0:T(1,128)}) custom-call(bf16[4,6,128,256]{3,2,1,0:T(8,128)(2,1)} %copy.109.q_ref, bf16[2048,512]{1,0:T(8,128)(2,1)} %get-tuple-element.29.k_ref, bf16[2048,512]{1,0:T(8,128)(2,1)} %get-tuple-element.30.v_ref, s32[2048,1]{1,0:T(8,128)} %copy.110.kdoc_ref, s32[2048,1]{1,0:T(8,128)} %copy.111.kplace_ref, ...), custom_call_target="tpu_custom_call" | custom-call | flops 6442450944 | bytes 16777216 | tf_op jit(solution)/shard_map/attend/pallas_call | solution.py:190
  163.3 81.6 %gather_tokens.1 = (bf16[2048,1536]{1,0:T(8,128)(2,1)}, f32[128,256]{1,0:T(8,128)}) custom-call(bf16[256,1536]{1,0:T(8,128)(2,1)} %copy-done.6, f32[16,256]{1,0:T(8,128)} %fusion.49.refs_1_), custom_call_target="tpu_custom_call" | custom-call | bytes 104857600 | tf_op jit(solution)/shard_map/gather_tokens/pallas_call | solution.py:447
  247.2 65.8 %all-gather.21.cloned.1.call-done = bf16[1,2048,1536]{2,1,0:T(8,128)(2,1)} async-done(((bf16[1,256,1536]{2,1,0:T(8,128)(2,1)}), bf16[1,2048,1536]{2,1,0:T(8,128)(2,1)}) %all-gather.21.cloned.1.call-update) | async-done | bytes 6291472 | tf_op jit(solution)/shard_map/all_gather | solution.py:578
  313.0 102.4 %experts.1 = (bf16[2048,1536]{1,0:T(8,128)(2,1)}, bf16[2048,1536]{1,0:T(8,128)(2,1)}, f32[2048,2]{1,0:T(8,128)}, bf16[2,1536,1024]{2,1,0:T(8,128)(2,1)}, bf16[2,512,1536]{2,1,0:T(8,128)(2,1)}) custom-call(bf16[2048,1536]{1,0:T(8,128)(2,1)} %get-tuple-element.32.x_ref, bf16[2048,1536]{1,0:T(8,128)(2,1)} %bitcast.205, f32[2048,2]{1,0:T(8,128)} %bitcast.189, ...), custom_call_target="tpu_custom_call" | custom-call | flops 57982058496 | bytes 50331648 | tf_op jit(solution)/shard_map/experts/pallas_call | solution.py:303
  417.5 116.1 %scatter_rows.1 = (f32[256,1536]{1,0:T(8,128)S(1)}, f32[16,256]{1,0:T(8,128)S(1)}) custom-call(bf16[2048,1536]{1,0:T(8,128)(2,1)} %get-tuple-element.35.refs_0_, f32[128,256]{1,0:T(8,128)S(1)} %bitcast.166), custom_call_target="tpu_custom_call" | custom-call | bytes 104857600 | tf_op jit(solution)/shard_map/scatter_rows/pallas_call | solution.py:523
  536.1 46.4 %reduce-scatter.12.cloned.1.call-done = bf16[256,1536]{1,0:T(8,128)(2,1)} async-done(((bf16[2048,1536]{1,0:T(8,128)(2,1)}), bf16[256,1536]{1,0:T(8,128)(2,1)}) %reduce-scatter.12.cloned.1.call-update) | async-done | bytes 786448 | tf_op jit(solution)/shard_map/reduce_scatter | solution.py:646
  586.2 4.9 convert_multiply_fusion.1
  605.5 41.3 %attend_back.1 = (f32[4,6,128,256]{3,2,1,0:T(8,128)}, bf16[2048,512]{1,0:T(8,128)(2,1)}, bf16[2048,512]{1,0:T(8,128)(2,1)}) custom-call(bf16[4,6,128,256]{3,2,1,0:T(8,128)(2,1)} %copy.109.q_ref, bf16[4,6,256,128]{3,2,1,0:T(8,128)(2,1)} %bitcast.172, bf16[4,6,128,256]{3,2,1,0:T(8,128)(2,1)} %copy.122.g_ref, bf16[4,6,256,128]{3,2,1,0:T(8,128)(2,1)} %bitcast.174, ...), custom_call_target="tpu_custom_call" | custom-call | flops 16106127360 | bytes 25165824 | tf_op jit(solution)/shard_map/attend_back/pallas_call | solution.py:212
  650.0 42.5 %scatter_keys.1 = (f32[256,512]{1,0:T(8,128)S(1)}, f32[256,512]{1,0:T(8,128)S(1)}) custom-call(bf16[2048,512]{1,0:T(8,128)(2,1)S(1)} %copy-done, bf16[2048,512]{1,0:T(8,128)(2,1)S(1)} %copy-done.1), custom_call_target="tpu_custom_call" | custom-call | bytes 104857600 | tf_op jit(solution)/shard_map/scatter_keys/pallas_call | solution.py:523
  698.0 4.6 copy.132
  702.7 5.0 convolution_convert_fusion
  726.3 14.7 %reduce-scatter.24.cloned.1.call-done = bf16[384,1024]{1,0:T(8,128)(2,1)} async-done(((bf16[1536,1024]{1,0:T(8,128)(2,1)}), bf16[384,1024]{1,0:T(8,128)(2,1)}) %reduce-scatter.24.cloned.1.call-update) | async-done | bytes 786448
  743.2 48.1 %reduce-scatter.16.cloned.1.call-done = bf16[384,1536]{1,0:T(8,128)(2,1)} async-done(((bf16[1536,1536]{1,0:T(8,128)(2,1)}), bf16[384,1536]{1,0:T(8,128)(2,1)}) %reduce-scatter.16.cloned.1.call-update) | async-done | bytes 1179664 | tf_op jit(solution)/shard_map/reduce_scatter | solution.py:705
  791.4 50.5 %reduce-scatter.14.cloned.1.call-done = bf16[384,1536]{1,0:T(8,128)(2,1)} async-done(((bf16[1536,1536]{1,0:T(8,128)(2,1)}), bf16[384,1536]{1,0:T(8,128)(2,1)}) %reduce-scatter.14.cloned.1.call-update) | async-done | bytes 1179664 | tf_op jit(solution)/shard_map/reduce_scatter | solution.py:705
  841.9 40.9 %reduce-scatter.20.cloned.1.call-done = bf16[2,128,1536]{2,1,0:T(8,128)(2,1)} async-done(((bf16[2,512,1536]{2,1,0:T(8,128)(2,1)}), bf16[2,128,1536]{2,1,0:T(8,128)(2,1)}) %reduce-scatter.20.cloned.1.call-update) | async-done | bytes 786448 | tf_op jit(solution)/shard_map/reduce_scatter | solution.py:705
  885.2 59.0 %reduce-scatter.18.cloned.1.call-done = bf16[2,384,1024]{2,1,0:T(8,128)(2,1)} async-done(((bf16[2,1536,1024]{2,1,0:T(8,128)(2,1)}), bf16[2,384,1024]{2,1,0:T(8,128)(2,1)}) %reduce-scatter.18.cloned.1.call-update) | async-done | bytes 1572880 | tf_op jit(solution)/shard_map/reduce_scatter | solution.py:705
  949.5 18.5 %reduce-scatter.22.cloned.1.call-done = bf16[384,18]{1,0:T(8,128)(2,1)} async-done(((bf16[1536,18]{1,0:T(8,128)(2,1)}), bf16[384,18]{1,0:T(8,128)(2,1)}) %reduce-scatter.22.cloned.1.call-update) | async-done | bytes 13840
  969.0 39.2 %psum.28 = bf16[384,18]{0,1:T(8,128)(2,1)S(1)} all-reduce(bf16[384,18]{0,1:T(8,128)(2,1)S(1)} %copy.131), channel_id=1, replica_groups=mesh['ctx'=8,'wsh'=4] {'ctx'}, use_global_device_ids=true, to_apply=%region_16.17 | all-reduce | flops 6912 | bytes 27648 | tf_op jit(solution)/shard_map/psum | solution.py:708
  1009.4 92.3 %all-reduce.7.cloned.1.call-done = (bf16[384,1024]{0,1:T(8,128)(2,1)}, bf16[384,1536]{1,0:T(8,128)(2,1)}, bf16[384,1536]{1,0:T(8,128)(2,1)}) async-done(((bf16[384,1024]{0,1:T(8,128)(2,1)}, bf16[384,1536]{1,0:T(8,128)(2,1)}, bf16[384,1536]{1,0:T(8,128)(2,1)}), (bf16[384,1024]{0,1:T(8,128)(2,1)}, bf16[384,1536]{1,0:T(8,128)(2,1)}, bf16[384,1536]{1,0:T(8,128)(2,1)})) %all-reduce.7.cloned.1.call-update) | async-done | bytes 3145744 | tf_op jit(solution)/shard_map/psum | solution.py:708
  (188 shorter events, 106.2 us)
Async XLA Ops:
  7.2 24.8 %all-gather.11.cloned.1.call-start = ((), (), s32[]{:S(2)}) async-start(), calls=%async_computation.8 | async-start | bytes 1966080 | tf_op jit(solution)/shard_map/all_gather | solution.py:565
  7.9 45.4 %all-gather.13.cloned.1.call-start = ((), (), s32[]{:S(2)}) async-start(), calls=%async_computation.9 | async-start | bytes 1966080 | tf_op jit(solution)/shard_map/all_gather | solution.py:565
  8.7 94.3 %all-gather.9.cloned.1.call-start = ((), (), s32[]{:S(2)}) async-start(), calls=%async_computation.7 | async-start | bytes 5898240 | tf_op jit(solution)/shard_map/all_gather | solution.py:565
  9.4 147.7 %all-gather.15.cloned.1.call-start = ((), (), s32[]{:S(2)}) async-start(), calls=%async_computation.10 | async-start | bytes 5898240 | tf_op jit(solution)/shard_map/all_gather | solution.py:565
  10.0 237.2 %all-gather.19.cloned.1.call-start = ((), (), s32[]{:S(2)}) async-start(), calls=%async_computation.12 | async-start | bytes 3932160 | tf_op jit(solution)/shard_map/all_gather | solution.py:565
  10.6 236.6 %all-gather.17.cloned.1.call-start = ((), (), s32[]{:S(2)}) async-start(), calls=%async_computation.11 | async-start | bytes 7864320 | tf_op jit(solution)/shard_map/all_gather | solution.py:565
  11.2 11.5 %copy-start.2 = (bf16[1,256,1536]{2,1,0:T(8,128)(2,1)S(1)}, bf16[1,256,1536]{2,1,0:T(8,128)(2,1)}, u32[]{:S(2)}) copy-start(bf16[1,256,1536]{2,1,0:T(8,128)(2,1)} %param.14) | copy-start | bytes 2359300
  11.2 301.8 %all-gather.21.cloned.1.call-start = ((), (), s32[]{:S(2)}) async-start(), calls=%async_computation.18 | async-start | bytes 7077888 | tf_op jit(solution)/shard_map/all_gather | solution.py:578
  12.0 570.6 %reduce-scatter.12.cloned.1.call-start = ((), (), s32[]{:S(2)}) async-start(), calls=%async_computation.13 | async-start | bytes 7077888 | tf_op jit(solution)/shard_map/reduce_scatter | solution.py:646
  23.0 86.7 %copy-start.18 = (f32[256]{0:T(256)}, f32[256]{0:T(256)S(1)}, u32[]{:S(2)}) copy-start(f32[256]{0:T(256)S(1)} %add_rsqrt_fusion.1) | copy-start | bytes 3076
  157.0 258.5 %copy-start.3 = (f32[4,2,3,64,256]{4,3,2,1,0:T(8,128)}, f32[4,2,3,64,256]{4,3,2,1,0:T(8,128)S(1)}, u32[]{:S(2)}) copy-start(f32[4,2,3,64,256]{4,3,2,1,0:T(8,128)S(1)} %pad_maximum_fusion.2) | copy-start | bytes 4718596
  162.7 371.0 %copy-start.21 = (f32[256]{0:T(256)}, f32[256]{0:T(256)S(1)}, u32[]{:S(2)}) copy-start(f32[256]{0:T(256)S(1)} %get-tuple-element.129) | copy-start | bytes 3076
  162.7 370.9 %copy-start.24 = (f32[256]{0:T(256)}, f32[256]{0:T(256)S(1)}, u32[]{:S(2)}) copy-start(f32[256]{0:T(256)S(1)} %fusion.44) | copy-start | bytes 3076
  415.5 325.5 %reduce-scatter.24.cloned.1.call-start = ((), (), s32[]{:S(2)}) async-start(), calls=%async_computation.20 | async-start | bytes 3932160
  417.5 116.9 %copy-start.5 = (f32[256,1536]{1,0:T(8,128)S(1)}, f32[256,1536]{1,0:T(8,128)}, u32[]{:S(2)}) copy-start(f32[256,1536]{1,0:T(8,128)} %copy-done.4) | copy-start | bytes 4718596
  417.5 116.9 %copy-start.23 = (f32[256]{0:T(256)S(1)}, f32[256]{0:T(256)}, u32[]{:S(2)}) copy-start(f32[256]{0:T(256)} %copy-done.22) | copy-start | bytes 3076
  534.4 48.1 %copy-start.11 = (bf16[1,256,1536]{2,1,0:T(8,128)(2,1)S(1)}, bf16[1,256,1536]{2,1,0:T(8,128)(2,1)}, u32[]{:S(2)}) copy-start(bf16[1,256,1536]{2,1,0:T(8,128)(2,1)} %param.27) | copy-start | bytes 2359300
  650.0 43.6 %copy-start.17 = (f32[256,32]{0,1:T(8,128)S(1)}, f32[256,32]{0,1:T(8,128)}, u32[]{:S(2)}) copy-start(f32[256,32]{0,1:T(8,128)} %get-tuple-element.124) | copy-start | bytes 98308
  702.6 88.7 %reduce-scatter.16.cloned.1.call-start = ((), (), s32[]{:S(2)}) async-start(), calls=%async_computation.15 | async-start | bytes 5898240 | tf_op jit(solution)/shard_map/reduce_scatter | solution.py:705
  707.7 134.2 %reduce-scatter.14.cloned.1.call-start = ((), (), s32[]{:S(2)}) async-start(), calls=%async_computation.14 | async-start | bytes 5898240 | tf_op jit(solution)/shard_map/reduce_scatter | solution.py:705
  714.8 168.0 %reduce-scatter.20.cloned.1.call-start = ((), (), s32[]{:S(2)}) async-start(), calls=%async_computation.17 | async-start | bytes 3932160 | tf_op jit(solution)/shard_map/reduce_scatter | solution.py:705
  715.4 228.8 %reduce-scatter.18.cloned.1.call-start = ((), (), s32[]{:S(2)}) async-start(), calls=%async_computation.16 | async-start | bytes 7864320 | tf_op jit(solution)/shard_map/reduce_scatter | solution.py:705
  716.1 251.8 %reduce-scatter.22.cloned.1.call-start = ((), (), s32[]{:S(2)}) async-start(), calls=%async_computation.19 | async-start | bytes 491520
  726.3 375.5 %all-reduce.7.cloned.1.call-start = ((), (), s32[]{:S(2)}) async-start(), calls=%async_computation.21 | async-start | bytes 6291456 | tf_op jit(solution)/shard_map/psum | solution.py:708
  (21 other events, 53.9 us)
Sparse Core Ops, SparseCore 0:
  9.5 22.3 all-gather.10
  33.5 19.8 all-gather.12
  54.9 37.4 all-gather.8
  93.8 37.4 all-gather.14
  132.7 28.5 all-gather.18
  162.6 46.3 all-gather.16
  211.2 101.7 all-gather.20
  415.6 166.8 reduce-scatter.11
  702.8 38.1 reduce-scatter.23
  743.3 47.9 reduce-scatter.15
  793.9 47.9 reduce-scatter.13
  844.9 37.8 reduce-scatter.19
  885.3 58.8 reduce-scatter.17
  947.1 20.8 reduce-scatter.21
  972.3 129.3 all-reduce.6

commit v2 on v1

--- a/solution.py
+++ b/solution.py
@@ -538,6 +538,207 @@
     )(*arrays)
 
 
+EXTRA = 16
+
+
+def reduce_kernel(
+    size, shards, lhs, rhs, small, out, part, cores, lines, total, stage, land, held,
+    core_send, core_recv, line_send, line_recv, ring_send, ring_recv, all_send, all_recv,
+):
+    ring = Ring(size)
+    steps, height = ring.steps, shards // 2
+    spot = lax.axis_index("wsh")
+    core, row = lax.rem(spot, 2), lax.div(spot, 2)
+    ctx = ring.me
+    slot_rows, width = total.shape[1], total.shape[2]
+    shard_rows = slot_rows - EXTRA
+    split = width // CHUNKS
+    mate = (ctx, row * 2 + 1 - core)
+    above = (ctx, lax.rem(row + 1, height) * 2 + core)
+    below = (ctx, lax.rem(row + height - 1, height) * 2 + core)
+
+    barrier = pltpu.get_barrier_semaphore()
+    for device in (mate, above, below, ring.device(0), ring.device(1)):
+        pl.semaphore_signal(barrier, inc=1, device_id=device, device_id_type=MESH)
+    pl.semaphore_wait(barrier, 5)
+
+    order = [steps]
+    for distance in range(steps - 1, 0, -1):
+        order += [distance, -distance]
+    order.append(0)
+    slot_of = {shift: i for i, shift in enumerate(order)}
+    slot_of[-steps] = 0
+    blocks = [ring.at(shift) for shift in order]
+    started = []
+
+    def begin(copy):
+        copy.start()
+        started.append(copy)
+
+    def remote(source, target, send, recv, device):
+        return pltpu.make_async_remote_copy(
+            src_ref=source,
+            dst_ref=target,
+            send_sem=send,
+            recv_sem=recv,
+            device_id=device,
+            device_id_type=MESH,
+        )
+
+    def to_mate(i, y):
+        return remote(
+            part.at[i, y * 2 + 1 - core], cores.at[i, y], core_send.at[i, y], core_recv.at[i, y], mate
+        )
+
+    def to_line(i, t):
+        shard = lax.rem(row + 2 * height - 1 - t, height) * 2 + core
+        return remote(
+            part.at[i, shard], lines.at[i, t], line_send.at[i, t], line_recv.at[i, t], above
+        )
+
+    def form(i):
+        at = pl.multiple_of(blocks[i] * width, width)
+        side = lax.div(blocks[i] * width, lhs.shape[1] + 2 * KEY_HEADS * HEAD_SIZE)
+
+        @pl.loop(0, shards)
+        def _(w):
+            rows = pl.ds(pl.multiple_of(w * shard_rows, shard_rows), shard_rows)
+            product = dot(lhs[side, rows, :], rhs[:, pl.ds(at, width)])
+            part[i, w, :shard_rows, :] = product.astype(BF16)
+            part[i, w, shard_rows:, :] = small[w, :, pl.ds(at, width)]
+
+        for y in range(height):
+            begin(to_mate(i, y))
+
+    def add_cores(i):
+        for y in range(height):
+            to_mate(i, y).wait_recv()
+            both = part[i, y * 2 + core].astype(F32) + cores[i, y].astype(F32)
+            part[i, y * 2 + core] = both.astype(BF16)
+        begin(to_line(i, 0))
+
+    for i in range(size):
+        form(i)
+        if i > 0:
+            add_cores(i - 1)
+    add_cores(size - 1)
+    for t in range(1, height - 1):
+        for i in range(size):
+            to_line(i, t - 1).wait_recv()
+            shard = lax.rem(row + 2 * height - 1 - t, height) * 2 + core
+            both = part[i, shard].astype(F32) + lines[i, t - 1].astype(F32)
+            part[i, shard] = both.astype(BF16)
+            begin(to_line(i, t))
+
+    def finish_line(i):
+        to_line(i, height - 2).wait_recv()
+        total[i] = part[i, spot].astype(F32) + lines[i, height - 2].astype(F32)
+
+    def columns(chunk):
+        return pl.ds(chunk * split, split)
+
+    def around(direction, step, chunk):
+        return remote(
+            stage.at[direction, step, :, columns(chunk)],
+            land.at[direction, step, :, columns(chunk)],
+            ring_send.at[direction, step, chunk],
+            ring_recv.at[direction, step, chunk],
+            ring.device(direction),
+        )
+
+    for step in range(steps):
+        reach = steps - step
+        for i in sorted({slot_of[reach], slot_of[-reach]}):
+            finish_line(i)
+        for chunk in range(CHUNKS):
+            for direction in range(2):
+                if step == 0 and chunk not in ring.chunks(direction, True):
+                    continue
+                at = columns(chunk)
+                value = total[slot_of[reach if direction == 0 else -reach], :, at]
+                if step > 1 or (step == 1 and chunk in ring.chunks(direction, True)):
+                    around(direction, step - 1, chunk).wait_recv()
+                    value += land[direction, step - 1, :, at].astype(F32)
+                stage[direction, step, :, at] = value.astype(BF16)
+                begin(around(direction, step, chunk))
+
+    def onward(direction, step, chunk, block):
+        return remote(
+            held.at[block, :, columns(chunk)],
+            held.at[block, :, columns(chunk)],
+            all_send.at[direction, step, chunk],
+            all_recv.at[direction, step, chunk],
+            ring.device(direction),
+        )
+
+    def put(block, chunk):
+        at = pl.ds(pl.multiple_of(block * width + chunk * split, split), split)
+        out[:, at] = held[block, :, columns(chunk)].astype(F32)
+
+    own = slot_of[0]
+    finish_line(own)
+    for chunk in range(CHUNKS):
+        at = columns(chunk)
+        value = total[own, :, at]
+        for direction in range(2):
+            around(direction, steps - 1, chunk).wait_recv()
+            value += land[direction, steps - 1, :, at].astype(F32)
+        held[ctx, :, at] = value.astype(BF16)
+        for direction in range(2):
+            begin(onward(direction, 0, chunk, ctx))
+    for chunk in range(CHUNKS):
+        put(ctx, chunk)
+    for step in range(1, steps + 1):
+        for chunk in range(CHUNKS):
+            for direction in range(2):
+                if step == steps and chunk not in ring.chunks(direction, True):
+                    continue
+                block = ring.toward(1 - direction, step)
+                onward(direction, step - 1, chunk, block).wait_recv()
+                if step < steps and chunk in ring.chunks(direction, step == steps - 1):
+                    begin(onward(direction, step, chunk, block))
+                put(block, chunk)
+    for copy in started:
+        copy.wait_send()
+
+
+def reduce_grads(lhs, rhs, small, size, shards, identity):
+    steps, height = size // 2, shards // 2
+    columns = rhs.shape[1]
+    width, rows = columns // size, lhs.shape[1] // shards + EXTRA
+    vmem = pl.BlockSpec(memory_space=pltpu.VMEM)
+    dma = pltpu.SemaphoreType.DMA
+    return pl.pallas_call(
+        functools.partial(reduce_kernel, size, shards),
+        in_specs=[vmem] * 3,
+        out_specs=vmem,
+        out_shape=jax.ShapeDtypeStruct((rows, columns), F32),
+        scratch_shapes=[
+            pltpu.VMEM((size, shards, rows, width), BF16),
+            pltpu.VMEM((size, height, rows, width), BF16),
+            pltpu.VMEM((size, height - 1, rows, width), BF16),
+            pltpu.VMEM((size, rows, width), F32),
+            pltpu.VMEM((2, steps, rows, width), BF16),
+            pltpu.VMEM((2, steps, rows, width), BF16),
+            pltpu.VMEM((size, rows, width), BF16),
+            dma((size, height)),
+            dma((size, height)),
+            dma((size, height - 1)),
+            dma((size, height - 1)),
+        ]
+        + [dma((2, steps, CHUNKS))] * 4,
+        compiler_params=pltpu.CompilerParams(
+            collective_id=identity, has_side_effects=True, vmem_limit_bytes=62 << 20
+        ),
+        cost_estimate=pl.CostEstimate(
+            flops=2 * lhs.shape[1] * lhs.shape[2] * columns,
+            bytes_accessed=300 << 20,
+            transcendentals=0,
+        ),
+        name="reduce_grads",
+    )(lhs, rhs, small)
+
+
 def on_device(
     layer_input,
     attention_gain,
@@ -655,7 +856,6 @@
     gain_two_grad, residual_back = norm_backward(residual, inverse_two, gain_two, normed_two_grad)
     residual_grad = out_grad + residual_back
     branch_grad = residual_grad.astype(BF16)
-    output_grad = dot_tn(attended, branch_grad)
     attended_grad = dot_nt(branch_grad, whole_output).astype(BF16)
     delta = jnp.sum(
         (attended_grad.astype(F32) * attended_f).reshape(token_rows, QUERY_HEADS, HEAD_SIZE), axis=-1
@@ -690,9 +890,6 @@
         .reshape(token_rows, key_value_width)
         .astype(BF16)
     )
-    query_weight_grad = dot_tn(normed_one, query_pre_grad)
-    key_weight_grad = dot_tn(normed_one, key_pre_grad)
-    value_weight_grad = dot_tn(normed_one, value_grad)
     normed_one_grad = (
         dot_nt(query_pre_grad, whole_query)
         + dot_nt(key_pre_grad, whole_key)
@@ -704,27 +901,48 @@
     def scatter(grad, dim=0):
         return lax.psum_scatter(grad.astype(BF16), "wsh", scatter_dimension=dim, tiled=True)
 
-    def reduce(grad):
-        return lax.psum(scatter(grad), "ctx").astype(F32)
-
     inner_out = scatter(inner_grad, 1).astype(F32)
     outer_out = scatter(outer_grad, 1).astype(F32)
-    output_out = reduce(output_grad)
-    query_out = reduce(query_weight_grad)
-    key_value_out = reduce(jnp.concatenate([key_weight_grad, value_weight_grad], axis=1))
-    small_out = reduce(
-        jnp.concatenate([gain_one_grad[:, None], gain_two_grad[:, None], router_grad], axis=1)
+    shards = lax.axis_size("wsh")
+    shard_rows = query_weight.shape[0]
+    columns = 2 * query_weight.shape[1] + 2 * key_value_width
+    marks_small = jnp.concatenate(
+        [gain_one_grad[None], gain_two_grad[None], router_grad.T], axis=0
+    ).astype(BF16)
+    small_count = marks_small.shape[0]
+    small_rows = marks_small.reshape(small_count, shards, shard_rows).transpose(1, 0, 2)
+    small_rows = small_rows.reshape(shards, small_count * shard_rows)
+    across = -(-small_count * shard_rows // EXTRA // 128) * 128
+    small_rows = jnp.pad(small_rows, ((0, 0), (0, EXTRA * across - small_rows.shape[1])))
+    small_rows = jnp.pad(
+        small_rows.reshape(shards, EXTRA, across), ((0, 0), (0, 0), (0, columns - across))
+    )
+    summed = reduce_grads(
+        jnp.stack([normed_one.T, attended.T]),
+        jnp.concatenate([query_pre_grad, key_pre_grad, value_grad, branch_grad], axis=1),
+        small_rows,
+        group_devices,
+        shards,
+        5,
+    )
+    small_out = summed[shard_rows:, :across].reshape(-1)[: small_count * shard_rows]
+    small_out = small_out.reshape(small_count, shard_rows)
+    ends = [0]
+    for shard in (query_weight, key_matrix, value_matrix, output_weight):
+        ends.append(ends[-1] + shard.shape[1])
+    query_out, key_out, value_out, output_out = (
+        summed[:shard_rows, start:end] for start, end in zip(ends, ends[1:])
     )
     return (
         layer_output[None],
         input_grad[None],
-        small_out[:, 0],
+        small_out[0],
         query_out,
-        key_value_out[:, :key_value_width],
-        key_value_out[:, key_value_width:],
+        key_out,
+        value_out,
         output_out,
-        small_out[:, 1],
-        small_out[:, 2:],
+        small_out[1],
+        small_out[2:].T,
         inner_out,
         outer_out,
     )

time: 1130 us -> 807 us (0.71)
  waiting for transfers between devices: 468 us -> 97.1 us
  Pallas kernels: 465 us -> 571 us
  blocking collectives: 45.5 us -> 6.29 us
  matrix products: 36.8 us -> 23.9 us
    reduce_scatter x4 -> x2, waiting for transfers between devices: 198 us -> 0.01 us  [scatter(): lax.psum_scatter(grad.astype(BF16), 'wsh', scatter_dimension=dim, tiled=T...]
    pallas_call x0 -> x1, Pallas kernels: none -> 118 us  [reduce_grads(): pl.pallas_call(functools.partial(reduce_kernel, size, shards), in_specs=[...]
    psum x1 -> x0, waiting for transfers between devices: 92.3 us -> none  [reduce(): return lax.psum(scatter(grad), 'ctx').astype(F32)]
    reduce_scatter x1, waiting for transfers between devices: 46.4 us -> 0.01 us  [on_device(): mixture = lax.psum_scatter(mixed, 'ctx', scatter_dimension=0, tiled=True)]
    psum x1 -> x0, blocking collectives: 39.2 us -> none  [reduce(): return lax.psum(scatter(grad), 'ctx').astype(F32)]
    unnamed x17 -> x10, waiting for transfers between devices: 38.8 us -> 5.55 us
    pallas_call x2, Pallas kernels: 159 us -> 145 us  [ring_scatter(): pl.pallas_call(functools.partial(ring_scatter_kernel, size, count), in_sp...]
  transfers between devices with their start and end apart: 15 -> 10, of which waited for: 11 -> 3; matrix products, arithmetic and copies ran while one was open for 7% -> 12% of each run, Pallas kernels for 25% -> 59%
where the time goes in v2:
time: 807 us; the launch traced here: 796 us
  Pallas kernels  571 us (71%)
  waiting for transfers between devices  97.1 us (12%)
  local copies, waits for them, and re-layouts  58.3 us (7%)
  other arithmetic  24.4 us (3%)
  matrix products  23.9 us (3%)
  between operations  15.1 us (2%)
    pallas_call x2, Pallas kernels, ring_scatter(): pl.pallas_call(functools.partial(ring_scatter_kernel, size, count), in_sp...  145 us
    pallas_call x2, Pallas kernels, ring_gather(): pl.pallas_call(functools.partial(ring_gather_kernel, size, count), in_spe...  129 us
    pallas_call x1, Pallas kernels, reduce_grads(): pl.pallas_call(functools.partial(reduce_kernel, size, shards), in_specs=[...  118 us
    pallas_call x1, Pallas kernels, experts_pass(): pl.pallas_call(expert_kernel, grid=(rows // block,), in_specs=[row_spec,...  102 us
    all_gather x1, waiting for transfers between devices, on_device(): all_grads = lax.all_gather(cotangent[0], 'ctx', axis=0, tiled=True)  64.8 us
    pallas_call x1, Pallas kernels, attend_back(): pl.pallas_call(attend_back_kernel, grid=(PAIRS, PAIR_HEADS), in_specs=[he...  41.4 us
    pallas_call x1, Pallas kernels, attend(): pl.pallas_call(attend_kernel, grid=(PAIRS, PAIR_HEADS), in_specs=[head, k...  34.4 us
    all_gather x6, waiting for transfers between devices, gather(): return lax.all_gather(shard, 'wsh', axis=axis, tiled=True)  26.8 us
  transfers between devices with their start and end apart: 10, of which 3 were waited for; matrix products, arithmetic and copies ran while one was open for 12% of the time, Pallas kernels for 59%

profile of v2, /device:TPU:0, one launch (start us, length us, event | category | flops | bytes accessed | tf_op | source)
XLA Modules:
  0.0 796.5 jit_solution(1150046779151747483)
XLA Ops:
  15.8 6.3 all_gather.24
  23.2 8.7 %all-gather.11.cloned.1.call-done = bf16[1536,512]{1,0:T(8,128)(2,1)} async-done(((bf16[384,512]{1,0:T(8,128)(2,1)}), bf16[1536,512]{1,0:T(8,128)(2,1)}) %all-gather.11.cloned.1.call-update) | async-done | bytes 1572880 | tf_op jit(solution)/shard_map/all_gather | solution.py:766
  35.3 18.0 %all-gather.13.cloned.1.call-done = bf16[1536,512]{1,0:T(8,128)(2,1)} async-done(((bf16[384,512]{1,0:T(8,128)(2,1)}), bf16[1536,512]{1,0:T(8,128)(2,1)}) %all-gather.13.cloned.1.call-update) | async-done | bytes 1572880 | tf_op jit(solution)/shard_map/all_gather | solution.py:766
  53.3 2.7 convolution_convert_fusion.2.refs_1_
  56.1 46.9 %gather_keys.1 = (bf16[2048,512]{1,0:T(8,128)(2,1)}, bf16[2048,512]{1,0:T(8,128)(2,1)}) custom-call(bf16[256,512]{1,0:T(8,128)(2,1)} %copy.83.refs_0_, bf16[256,512]{1,0:T(8,128)(2,1)} %convolution_convert_fusion.2.refs_1_), custom_call_target="tpu_custom_call" | custom-call | bytes 104857600 | tf_op jit(solution)/shard_map/gather_keys/pallas_call | solution.py:447
  103.0 6.7 copy.78
  109.7 3.9 fusion.25
  120.9 34.4 %attend.1 = (f32[4,6,128,256]{3,2,1,0:T(8,128)}, f32[4,6,1,256]{3,2,1,0:T(1,128)}) custom-call(bf16[4,6,128,256]{3,2,1,0:T(8,128)(2,1)} %copy.84.q_ref, bf16[2048,512]{1,0:T(8,128)(2,1)} %get-tuple-element.29.k_ref, bf16[2048,512]{1,0:T(8,128)(2,1)} %get-tuple-element.30.v_ref, s32[2048,1]{1,0:T(8,128)} %copy.85.kdoc_ref, s32[2048,1]{1,0:T(8,128)} %copy.86.kplace_ref, ...), custom_call_target="tpu_custom_call" | custom-call | flops 6442450944 | bytes 16777216 | tf_op jit(solution)/shard_map/attend/pallas_call | solution.py:190
  158.6 4.3 multiply_reduce_fusion.2
  164.2 82.6 %gather_tokens.1 = (bf16[2048,1536]{1,0:T(8,128)(2,1)}, f32[128,256]{1,0:T(8,128)}) custom-call(bf16[256,1536]{1,0:T(8,128)(2,1)} %copy-done.4, f32[16,256]{1,0:T(8,128)} %fusion.43.refs_1_), custom_call_target="tpu_custom_call" | custom-call | bytes 104857600 | tf_op jit(solution)/shard_map/gather_tokens/pallas_call | solution.py:447
  249.0 64.8 %all-gather.21.cloned.1.call-done = bf16[1,2048,1536]{2,1,0:T(8,128)(2,1)} async-done(((bf16[1,256,1536]{2,1,0:T(8,128)(2,1)}), bf16[1,2048,1536]{2,1,0:T(8,128)(2,1)}) %all-gather.21.cloned.1.call-update) | async-done | bytes 6291472 | tf_op jit(solution)/shard_map/all_gather | solution.py:779
  313.7 102.5 %experts.1 = (bf16[2048,1536]{1,0:T(8,128)(2,1)}, bf16[2048,1536]{1,0:T(8,128)(2,1)}, f32[2048,2]{1,0:T(8,128)}, bf16[2,1536,1024]{2,1,0:T(8,128)(2,1)}, bf16[2,512,1536]{2,1,0:T(8,128)(2,1)}) custom-call(bf16[2048,1536]{1,0:T(8,128)(2,1)} %get-tuple-element.32.x_ref, bf16[2048,1536]{1,0:T(8,128)(2,1)} %bitcast.226, f32[2048,2]{1,0:T(8,128)} %bitcast.204, ...), custom_call_target="tpu_custom_call" | custom-call | flops 57982058496 | bytes 50331648 | tf_op jit(solution)/shard_map/experts/pallas_call | solution.py:303
  418.6 102.5 %scatter_rows.1 = (f32[256,1536]{1,0:T(8,128)S(1)}, f32[16,256]{1,0:T(8,128)S(1)}) custom-call(bf16[2048,1536]{1,0:T(8,128)(2,1)} %get-tuple-element.35.refs_0_, f32[128,256]{1,0:T(8,128)S(1)} %bitcast.183), custom_call_target="tpu_custom_call" | custom-call | bytes 104857600 | tf_op jit(solution)/shard_map/scatter_rows/pallas_call | solution.py:523
  524.7 4.7 convolution_convert_fusion
  531.8 2.8 convert_bitcast_fusion.1
  543.7 41.4 %attend_back.1 = (f32[4,6,128,256]{3,2,1,0:T(8,128)}, bf16[2048,512]{1,0:T(8,128)(2,1)}, bf16[2048,512]{1,0:T(8,128)(2,1)}) custom-call(bf16[4,6,128,256]{3,2,1,0:T(8,128)(2,1)} %copy.84.q_ref, bf16[4,6,256,128]{3,2,1,0:T(8,128)(2,1)} %bitcast.186, bf16[4,6,128,256]{3,2,1,0:T(8,128)(2,1)} %copy.98.g_ref, bf16[4,6,256,128]{3,2,1,0:T(8,128)(2,1)} %bitcast.189, ...), custom_call_target="tpu_custom_call" | custom-call | flops 16106127360 | bytes 25165824 | tf_op jit(solution)/shard_map/attend_back/pallas_call | solution.py:212
  588.3 42.7 %scatter_keys.1 = (f32[256,512]{1,0:T(8,128)S(1)}, f32[256,512]{1,0:T(8,128)S(1)}) custom-call(bf16[2048,512]{1,0:T(8,128)(2,1)S(1)} %copy-done, bf16[2048,512]{1,0:T(8,128)(2,1)S(1)} %copy-done.1), custom_call_target="tpu_custom_call" | custom-call | bytes 104857600 | tf_op jit(solution)/shard_map/scatter_keys/pallas_call | solution.py:523
  638.2 3.9 fusion.49
  649.2 2.6 convert_element_type.132
  651.8 4.7 fusion.11
  658.2 118.2 %reduce_grads.1 = f32[400,4096]{1,0:T(8,128)} custom-call(bf16[2,1536,256]{2,1,0:T(8,128)(2,1)} %copy.106.lhs, bf16[256,4096]{1,0:T(8,128)(2,1)} %pad_maximum_fusion.rhs, bf16[4,16,4096]{2,1,0:T(8,128)(2,1)} %pad.13.small), custom_call_target="tpu_custom_call" | custom-call | flops 3221225472 | bytes 314572800 | tf_op jit(solution)/shard_map/reduce_grads/pallas_call | solution.py:711
  778.5 2.6 fusion.46
  781.1 4.9 fusion.45
  786.0 3.5 convert_element_type.131
  (168 shorter events, 65.3 us)
Async XLA Ops:
  7.2 24.8 %all-gather.11.cloned.1.call-start = ((), (), s32[]{:S(2)}) async-start(), calls=%async_computation.4 | async-start | bytes 1966080 | tf_op jit(solution)/shard_map/all_gather | solution.py:766
  7.9 45.4 %all-gather.13.cloned.1.call-start = ((), (), s32[]{:S(2)}) async-start(), calls=%async_computation.5 | async-start | bytes 1966080 | tf_op jit(solution)/shard_map/all_gather | solution.py:766
  8.7 94.3 %all-gather.9.cloned.1.call-start = ((), (), s32[]{:S(2)}) async-start(), calls=%async_computation.3 | async-start | bytes 5898240 | tf_op jit(solution)/shard_map/all_gather | solution.py:766
  9.4 149.2 %all-gather.15.cloned.1.call-start = ((), (), s32[]{:S(2)}) async-start(), calls=%async_computation.6 | async-start | bytes 5898240 | tf_op jit(solution)/shard_map/all_gather | solution.py:766
  10.0 2.2 copy-start.24
  10.0 2.2 copy-start.25
  10.0 2.2 copy-start.21
  10.0 239.0 %all-gather.19.cloned.1.call-start = ((), (), s32[]{:S(2)}) async-start(), calls=%async_computation.8 | async-start | bytes 3932160 | tf_op jit(solution)/shard_map/all_gather | solution.py:766
  10.6 238.4 %all-gather.17.cloned.1.call-start = ((), (), s32[]{:S(2)}) async-start(), calls=%async_computation.7 | async-start | bytes 7864320 | tf_op jit(solution)/shard_map/all_gather | solution.py:766
  11.2 4.6 copy-start.22
  11.2 11.5 %copy-start.23 = (s32[1,256,8]{1,2,0:T(8,128)S(1)}, s32[1,256,8]{1,2,0:T(8,128)}, u32[]{:S(2)}) copy-start(s32[1,256,8]{1,2,0:T(8,128)} %param.26) | copy-start | bytes 24580
  11.2 11.6 %copy-start.6 = (bf16[1,256,1536]{2,1,0:T(8,128)(2,1)S(1)}, bf16[1,256,1536]{2,1,0:T(8,128)(2,1)}, u32[]{:S(2)}) copy-start(bf16[1,256,1536]{2,1,0:T(8,128)(2,1)} %param.14) | copy-start | bytes 2359300
  11.2 302.5 %all-gather.21.cloned.1.call-start = ((), (), s32[]{:S(2)}) async-start(), calls=%async_computation.12 | async-start | bytes 7077888 | tf_op jit(solution)/shard_map/all_gather | solution.py:779
  12.0 637.3 %reduce-scatter.8.cloned.1.call-start = ((), (), s32[]{:S(2)}) async-start(), calls=%async_computation.11 | async-start | bytes 3932160 | tf_op jit(solution)/shard_map/reduce_scatter | solution.py:902
  416.2 235.6 %reduce-scatter.4.cloned.1.call-start = ((), (), s32[]{:S(2)}) async-start(), calls=%async_computation.9 | async-start | bytes 7077888 | tf_op jit(solution)/shard_map/reduce_scatter | solution.py:847
  417.0 369.0 %reduce-scatter.6.cloned.1.call-start = ((), (), s32[]{:S(2)}) async-start(), calls=%async_computation.10 | async-start | bytes 7864320 | tf_op jit(solution)/shard_map/reduce_scatter | solution.py:902
  418.6 102.6 %copy-start.5 = (bf16[256,1536]{1,0:T(8,128)(2,1)S(1)}, bf16[256,1536]{1,0:T(8,128)(2,1)}, u32[]{:S(2)}) copy-start(bf16[256,1536]{1,0:T(8,128)(2,1)} %copy-done.4) | copy-start | bytes 2359300
  529.4 2.4 copy-start.13
  635.0 2.6 copy-start.11
  638.2 3.9 copy-start.9
  638.2 3.9 copy-start.17
  643.8 2.9 copy-start.16
  649.2 2.6 copy-start.3
  651.8 4.7 copy-start.14
  (13 other events, 18.7 us)
Sparse Core Ops, SparseCore 0:
  9.5 22.3 all-gather.10
  33.5 19.8 all-gather.12
  54.9 37.4 all-gather.8
  93.8 37.4 all-gather.14
  132.7 28.4 all-gather.18
  162.6 46.3 all-gather.16
  211.2 102.4 all-gather.20
  416.3 36.0 reduce-scatter.7
  456.0 140.6 reduce-scatter.3
  599.1 61.5 reduce-scatter.5

commit v3 on v2

--- a/solution.py
+++ b/solution.py
@@ -538,6 +538,278 @@
     )(*arrays)
 
 
+FUSED_BYTES = 52 << 20
+
+
+def fused_kernel(
+    size, x_in, gate_in, g_hbm, wi_hbm, wo_hbm, back_out, gate_out, mix_hbm, dwi_hbm, dwo_hbm,
+    x, gates, g, wi, wo, rows, mid, part, gate_part, land, gate_land,
+    out_send, out_recv, sum_send, sum_recv, local,
+):
+    ring = Ring(size)
+    steps, me = ring.steps, ring.me
+    block, width = x_in.shape
+    count = wi.shape[0]
+    experts = gate_in.shape[0]
+    tile = 256
+    loads = [
+        pltpu.make_async_copy(a, b, local.at[i])
+        for i, (a, b) in enumerate(((wi_hbm, wi), (g_hbm, g), (wo_hbm, wo)))
+    ]
+    for load in loads:
+        load.start()
+    ring.meet()
+    whole_arrays, own_arrays = (x, gates), (x_in, gate_in)
+
+    def remote(source, target, send, recv, direction):
+        return pltpu.make_async_remote_copy(
+            src_ref=source,
+            dst_ref=target,
+            send_sem=send,
+            recv_sem=recv,
+            device_id=ring.device(direction),
+            device_id_type=MESH,
+        )
+
+    def spread(k, direction, step, chunk, origin, first=False):
+        height = own_arrays[k].shape[0]
+        at = rows_at(origin, height, chunk)
+        source = own_arrays[k].at[rows_at(0, height, chunk)] if first else whole_arrays[k].at[at]
+        return remote(
+            source,
+            whole_arrays[k].at[at],
+            out_send.at[k, direction, step, chunk],
+            out_recv.at[k, direction, step, chunk],
+            direction,
+        )
+
+    for chunk in range(CHUNKS):
+        for direction in range(2):
+            for k in range(2):
+                spread(k, direction, 0, chunk, me, True).start()
+    x[pl.ds(pl.multiple_of(me * block, block), block), :] = x_in[...]
+    gates[pl.ds(pl.multiple_of(me * experts, experts), experts), :] = gate_in[...]
+    for load in loads:
+        load.wait()
+
+    lanes = lax.broadcasted_iota(jnp.int32, (block, experts), 1)
+
+    def backward_rows(origin):
+        at = pl.ds(pl.multiple_of(origin * block, block), block)
+        gate_at = pl.ds(pl.multiple_of(origin * experts, experts), experts)
+        turned = gates[gate_at, :].T
+        picked = jnp.zeros((block, experts), F32)
+        grad = g[at, :]
+        for e in range(count):
+            mine = lanes == me * count + e
+            weight = jnp.sum(jnp.where(mine, turned, 0.0), axis=1, keepdims=True)
+            gate_sum = jnp.zeros((block, 1), F32)
+            for low in range(0, EXPERT_H, tile):
+                gate = dot(x[at, :], wi[e, :, low : low + tile])
+                up = dot(x[at, :], wi[e, :, EXPERT_H + low : EXPERT_H + low + tile])
+                inward = dot_nt(grad, wo[e, low : low + tile, :])
+                sigmoid = 1.0 / (1.0 + jnp.exp(-gate))
+                silu = gate * sigmoid
+                hidden = (silu * up).astype(BF16).astype(F32)
+                gate_sum += jnp.sum(hidden * inward, axis=1, keepdims=True)
+                hidden_grad = weight * inward
+                to = e * EXPERT_H + low
+                mid[at, to : to + tile] = (weight * hidden).astype(BF16)
+                to = 2 * e * EXPERT_H + low
+                rows[at, to : to + tile] = (
+                    hidden_grad * up * sigmoid * (1.0 + gate * (1.0 - sigmoid))
+                ).astype(BF16)
+                to += EXPERT_H
+                rows[at, to : to + tile] = (hidden_grad * silu).astype(BF16)
+            picked = jnp.where(mine, gate_sum, picked)
+        gate_part[gate_at, :] = picked.T
+
+        @pl.loop(0, width // tile)
+        def _(t):
+            to = pl.ds(pl.multiple_of(t * tile, tile), tile)
+            back = 0.0
+            for e in range(count):
+                inner = rows[at, 2 * e * EXPERT_H : 2 * (e + 1) * EXPERT_H]
+                back += dot_nt(inner, wi[e, to, :])
+            part[at, to] = back.astype(BF16)
+
+    def visit(j, carry):
+        step = lax.div(j + 1, 2)
+        odd = lax.rem(j, 2)
+
+        @pl.when((odd == 1) & (j < size - 1))
+        def _():
+            for chunk in range(CHUNKS):
+                for direction in range(2):
+                    origin = ring.toward(1 - direction, step)
+                    for k in range(2):
+                        spread(k, direction, step - 1, chunk, origin).wait_recv()
+
+                    def forward():
+                        for k in range(2):
+                            spread(k, direction, step, chunk, origin).start()
+
+                    if chunk in ring.chunks(direction, True):
+                        forward()
+                    else:
+                        pl.when(step < steps - 1)(forward)
+
+        @pl.when(j == size - 1)
+        def _():
+            for direction in range(2):
+                for chunk in ring.chunks(direction, True):
+                    for k in range(2):
+                        origin = ring.toward(1 - direction, steps)
+                        spread(k, direction, steps - 1, chunk, origin).wait_recv()
+
+        backward_rows(ring.at(step * (1 - 2 * odd)))
+        return carry
+
+    lax.fori_loop(0, size, visit, 0)
+
+    parts, lands, outs = (part, gate_part), (land, gate_land), (back_out, gate_out)
+
+    def inward_copy(k, direction, step, chunk):
+        height = own_arrays[k].shape[0]
+        dest = ring.toward(direction, steps - step)
+        return remote(
+            parts[k].at[rows_at(dest, height, chunk)],
+            lands[k].at[direction, step, rows_at(0, height, chunk)],
+            sum_send.at[k, direction, step, chunk],
+            sum_recv.at[k, direction, step, chunk],
+            direction,
+        )
+
+    def inward_step(step):
+        for chunk in range(CHUNKS):
+            for direction in range(2):
+                near = chunk in ring.chunks(direction, True)
+                if step == 0 and not near:
+                    continue
+                for k in range(2):
+                    height = own_arrays[k].shape[0]
+                    if step > 1 or (step == 1 and near):
+                        inward_copy(k, direction, step - 1, chunk).wait_recv()
+                        at = rows_at(ring.toward(direction, steps - step), height, chunk)
+                        landed = lands[k][direction, step - 1, rows_at(0, height, chunk)]
+                        both = parts[k][at, :].astype(F32) + landed.astype(F32)
+                        parts[k][at, :] = both.astype(parts[k].dtype)
+                    inward_copy(k, direction, step, chunk).start()
+
+    def inner_gradient(t):
+        to = pl.ds(pl.multiple_of(t * tile, tile), tile)
+        for e in range(count):
+            inner = rows[:, 2 * e * EXPERT_H : 2 * (e + 1) * EXPERT_H]
+            wi[e, to, :] = dot_tn(x[:, to], inner).astype(BF16)
+
+    def outer_gradient(t):
+        e = lax.div(t, EXPERT_H // tile)
+        low = lax.rem(t, EXPERT_H // tile)
+        from_ = pl.ds(pl.multiple_of(t * tile, tile), tile)
+        to = pl.ds(pl.multiple_of(low * tile, tile), tile)
+        wo[e, to, :] = dot_tn(mid[:, from_], g[...]).astype(BF16)
+
+    def mixture(origin):
+        at = pl.ds(pl.multiple_of(origin * block, block), block)
+        mixed = 0.0
+        for e in range(count):
+            mixed += dot(mid[at, e * EXPERT_H : (e + 1) * EXPERT_H], wo[e])
+        x[at, :] = mixed.astype(BF16)
+
+    tiles = width // tile
+    cuts = [round(tiles * i / (steps - 1)) for i in range(steps)]
+    stores = [
+        pltpu.make_async_copy(a, b, local.at[i])
+        for i, (a, b) in enumerate(((wi, dwi_hbm), (x, mix_hbm), (wo, dwo_hbm)))
+    ]
+    for step in range(steps):
+        inward_step(step)
+        if step < steps - 1:
+            pl.loop(cuts[step], cuts[step + 1])(inner_gradient)
+        else:
+            stores[0].start()
+            for k in range(2):
+                for direction in range(2):
+                    for hop in range(steps):
+                        for chunk in ring.chunks(direction, hop == steps - 1):
+                            spread(k, direction, hop, chunk, me, hop == 0).wait_send()
+            pl.loop(0, size)(mixture)
+            stores[1].start()
+            pl.loop(0, count * EXPERT_H // tile)(outer_gradient)
+            stores[2].start()
+    for chunk in range(CHUNKS):
+        for k in range(2):
+            height = own_arrays[k].shape[0]
+            here = rows_at(0, height, chunk)
+            total = parts[k][rows_at(me, height, chunk), :].astype(F32)
+            for direction in range(2):
+                inward_copy(k, direction, steps - 1, chunk).wait_recv()
+                total += lands[k][direction, steps - 1, here].astype(F32)
+            outs[k][here, :] = total
+    for k in range(2):
+        for direction in range(2):
+            for step in range(steps):
+                for chunk in ring.chunks(direction, step == 0):
+                    inward_copy(k, direction, step, chunk).wait_send()
+    for store in stores:
+        store.wait()
+
+
+def fused_scratch(tokens, gates, inner, outer, size):
+    block, width = tokens.shape
+    count, steps = inner.shape[0], size // 2
+    rows, gate_rows = size * block, size * gates.shape[0]
+    return [
+        pltpu.VMEM((rows, width), BF16),
+        pltpu.VMEM((gate_rows, block), F32),
+        pltpu.VMEM((rows, width), BF16),
+        pltpu.VMEM(inner.shape, BF16),
+        pltpu.VMEM(outer.shape, BF16),
+        pltpu.VMEM((rows, 2 * count * EXPERT_H), BF16),
+        pltpu.VMEM((rows, count * EXPERT_H), BF16),
+        pltpu.VMEM((rows, width), BF16),
+        pltpu.VMEM((gate_rows, block), F32),
+        pltpu.VMEM((2, steps, block, width), BF16),
+        pltpu.VMEM((2, steps) + gates.shape, F32),
+    ]
+
+
+def fused_fits(*shapes):
+    return sum(r.dtype.itemsize * functools.reduce(lambda a, b: a * b, r.shape) for r in fused_scratch(*shapes)) <= FUSED_BYTES
+
+
+def fused_experts(tokens, gates, grads, inner, outer, size, identity):
+    block, width = tokens.shape
+    count, steps = inner.shape[0], size // 2
+    rows = size * block
+    vmem, hbm = pl.BlockSpec(memory_space=pltpu.VMEM), pl.BlockSpec(memory_space=pl.ANY)
+    sems = pltpu.SemaphoreType.DMA((2, 2, steps, CHUNKS))
+    return pl.pallas_call(
+        functools.partial(fused_kernel, size),
+        in_specs=[vmem, vmem, hbm, hbm, hbm],
+        out_specs=[vmem, vmem, hbm, hbm, hbm],
+        out_shape=[
+            jax.ShapeDtypeStruct(tokens.shape, F32),
+            jax.ShapeDtypeStruct(gates.shape, F32),
+            jax.ShapeDtypeStruct((rows, width), BF16),
+            jax.ShapeDtypeStruct(inner.shape, BF16),
+            jax.ShapeDtypeStruct(outer.shape, BF16),
+        ],
+        scratch_shapes=fused_scratch(tokens, gates, inner, outer, size)
+        + [sems] * 4
+        + [pltpu.SemaphoreType.DMA((3,))],
+        compiler_params=pltpu.CompilerParams(
+            collective_id=identity, has_side_effects=True, vmem_limit_bytes=63 << 20
+        ),
+        cost_estimate=pl.CostEstimate(
+            flops=18 * count * rows * width * EXPERT_H,
+            bytes_accessed=300 << 20,
+            transcendentals=rows * count * EXPERT_H,
+        ),
+        name="fused_experts",
+    )(tokens, gates, grads, inner, outer)
+
+
 EXTRA = 16
 
 
@@ -765,18 +1037,20 @@
     def gather(shard, axis=0):
         return lax.all_gather(shard, "wsh", axis=axis, tiled=True)
 
-    small = gather(
-        jnp.concatenate([attention_gain[:, None], expert_gain[:, None], router_weight], axis=1)
+    projected = 2 * key_value_width + query_weight.shape[1]
+    small = jnp.concatenate([attention_gain[:, None], expert_gain[:, None], router_weight], axis=1)
+    small = jnp.pad(small, ((0, 0), (0, -small.shape[1] % 128)))
+    first_weights = gather(
+        jnp.concatenate([query_weight, key_matrix, value_matrix, small], axis=1)
     )
-    gain_one, gain_two = small[:, 0].astype(F32), small[:, 1].astype(F32)
-    whole_router = small[:, 2:]
-    whole_key = gather(key_matrix)
-    whole_value = gather(value_matrix)
-    whole_query = gather(query_weight)
+    whole_qkv = first_weights[:, :projected]
+    gain_one = first_weights[:, projected].astype(F32)
+    gain_two = first_weights[:, projected + 1].astype(F32)
+    whole_router = first_weights[:, projected + 2 : projected + 2 + experts]
     whole_output = gather(output_weight)
     whole_inner = gather(expert_inner, 1)
     whole_outer = gather(expert_outer, 1)
-    all_grads = lax.all_gather(cotangent[0], "ctx", axis=0, tiled=True)
+    (all_grads,) = ring_gather([cotangent[0]], group_devices, 6, "gather_grads")
 
     places_all = token_places[0]
     key_documents, key_offsets = locate(document_lengths[0], places_all)
@@ -792,18 +1066,20 @@
     )
     cosine_rows, sine_table = angles_for(query_offsets)
 
-    inputs_f = layer_input[0].astype(F32)
+    own_input, all_grads = lax.optimization_barrier((layer_input[0], all_grads))
+    inputs_f = own_input.astype(F32)
     inverse_one = rms_inverse(inputs_f)
     normed_one = (inputs_f * inverse_one * gain_one).astype(BF16)
-    key_pre = dot(normed_one, whole_key)
+    pre = dot(normed_one, whole_qkv)
+    query_pre = pre[:, : -2 * key_value_width]
+    key_pre = pre[:, -2 * key_value_width : -key_value_width]
     keys = (
         apply_rotation(key_pre.reshape(token_rows, KEY_HEADS, HEAD_SIZE), cosine_rows, sine_table)
         .astype(BF16)
         .reshape(token_rows, key_value_width)
     )
-    values = dot(normed_one, whole_value).astype(BF16)
+    values = pre[:, -key_value_width:].astype(BF16)
     all_keys, all_values = ring_gather([keys, values], group_devices, 1, "gather_keys")
-    query_pre = dot(normed_one, whole_query)
     queries = (
         apply_rotation(
             query_pre.reshape(token_rows, QUERY_HEADS, HEAD_SIZE), cosine_rows, sine_table
@@ -822,31 +1098,34 @@
     routed = jnp.any(expert_routes[0][:, :, None] == expert_ids[None, None, :], axis=1)
     gates = jax.nn.softmax(jnp.where(routed, logits, -jnp.inf), axis=-1)
 
-    all_tokens, all_gates = ring_gather([normed_two, gates.T], group_devices, 2, "gather_tokens")
-    own_gates = (
-        lax.dynamic_slice_in_dim(
-            all_gates.reshape(group_devices, experts, token_rows),
+    turned_gates = gates.T
+    if fused_fits(normed_two, turned_gates, whole_inner, whole_outer, group_devices):
+        back_sum, gate_grad, mixed, inner_grad, outer_grad = fused_experts(
+            normed_two, turned_gates, all_grads, whole_inner, whole_outer, group_devices, 7
+        )
+    else:
+        all_tokens, all_gates = ring_gather([normed_two, turned_gates], group_devices, 2, "gather_tokens")
+        own_gates = (
+            lax.dynamic_slice_in_dim(
+                all_gates.reshape(group_devices, experts, token_rows),
+                ctx_index * own_experts,
+                own_experts,
+                axis=1,
+            )
+            .transpose(0, 2, 1)
+            .reshape(group_devices * token_rows, own_experts)
+        )
+        mixed, back_rows, own_gate_grad, inner_grad, outer_grad = experts_pass(
+            all_tokens, all_grads, own_gates, whole_inner, whole_outer
+        )
+        placed = lax.dynamic_update_slice_in_dim(
+            jnp.zeros((group_devices, experts, token_rows), F32),
+            own_gate_grad.reshape(group_devices, token_rows, own_experts).transpose(0, 2, 1),
             ctx_index * own_experts,
-            own_experts,
             axis=1,
-        )
-        .transpose(0, 2, 1)
-        .reshape(group_devices * token_rows, own_experts)
-    )
-    mixed, back_rows, own_gate_grad, inner_grad, outer_grad = experts_pass(
-        all_tokens, all_grads, own_gates, whole_inner, whole_outer
-    )
-    placed = lax.dynamic_update_slice_in_dim(
-        jnp.zeros((group_devices, experts, token_rows), F32),
-        own_gate_grad.reshape(group_devices, token_rows, own_experts).transpose(0, 2, 1),
-        ctx_index * own_experts,
-        axis=1,
-    ).reshape(group_devices * experts, token_rows)
-    back_sum, gate_grad = ring_scatter([back_rows, placed], group_devices, 3, "scatter_rows")
+        ).reshape(group_devices * experts, token_rows)
+        back_sum, gate_grad = ring_scatter([back_rows, placed], group_devices, 3, "scatter_rows")
     gate_grad = gate_grad.T
-    mixture = lax.psum_scatter(mixed, "ctx", scatter_dimension=0, tiled=True)
-    layer_output = (residual + mixture.astype(F32)).astype(BF16)
-
     out_grad = cotangent[0].astype(F32)
     logit_grad = (
         gates * (gate_grad - jnp.sum(gates * gate_grad, axis=-1, keepdims=True))
@@ -890,19 +1169,18 @@
         .reshape(token_rows, key_value_width)
         .astype(BF16)
     )
-    normed_one_grad = (
-        dot_nt(query_pre_grad, whole_query)
-        + dot_nt(key_pre_grad, whole_key)
-        + dot_nt(value_grad, whole_value)
-    )
+    pre_grad = jnp.concatenate([query_pre_grad, key_pre_grad, value_grad], axis=1)
+    normed_one_grad = dot_nt(pre_grad, whole_qkv)
     gain_one_grad, input_back = norm_backward(inputs_f, inverse_one, gain_one, normed_one_grad)
     input_grad = residual_grad + input_back
 
     def scatter(grad, dim=0):
         return lax.psum_scatter(grad.astype(BF16), "wsh", scatter_dimension=dim, tiled=True)
 
-    inner_out = scatter(inner_grad, 1).astype(F32)
-    outer_out = scatter(outer_grad, 1).astype(F32)
+    inner_out = scatter(inner_grad, 1)
+    outer_out = scatter(outer_grad, 1)
+    mixed, inner_out, outer_out = lax.optimization_barrier((mixed, inner_out, outer_out))
+    mixture = lax.psum_scatter(mixed, "ctx", scatter_dimension=0, tiled=True)
     shards = lax.axis_size("wsh")
     shard_rows = query_weight.shape[0]
     columns = 2 * query_weight.shape[1] + 2 * key_value_width
@@ -919,12 +1197,14 @@
     )
     summed = reduce_grads(
         jnp.stack([normed_one.T, attended.T]),
-        jnp.concatenate([query_pre_grad, key_pre_grad, value_grad, branch_grad], axis=1),
+        jnp.concatenate([pre_grad, branch_grad], axis=1),
         small_rows,
         group_devices,
         shards,
         5,
     )
+    mixture, summed = lax.optimization_barrier((mixture, summed))
+    layer_output = (residual + mixture.astype(F32)).astype(BF16)
     small_out = summed[shard_rows:, :across].reshape(-1)[: small_count * shard_rows]
     small_out = small_out.reshape(small_count, shard_rows)
     ends = [0]
@@ -943,8 +1223,8 @@
         output_out,
         small_out[1],
         small_out[2:].T,
-        inner_out,
-        outer_out,
+        inner_out.astype(F32),
+        outer_out.astype(F32),
     )
 
 

time: 807 us -> 733 us (0.908)
  Pallas kernels: 571 us -> 513 us
  local copies, waits for them, and re-layouts: 58.3 us -> 47 us
    reduce_scatter x2, waiting for transfers between devices: 0.01 us -> 97.9 us  [scatter(): lax.psum_scatter(grad.astype(BF16), 'wsh', scatter_dimension=dim, tiled=T...]
    pallas_call x2 -> x1, Pallas kernels: 145 us -> 67.4 us  [ring_scatter(): pl.pallas_call(functools.partial(ring_scatter_kernel, size, count), in_sp...]
    all_gather x1 -> x0, waiting for transfers between devices: 64.8 us -> none  [on_device(): all_grads = lax.all_gather(cotangent[0], 'ctx', axis=0, tiled=True)]
    pallas_call x1, Pallas kernels: 102 us -> 140 us  [fused_experts(): pl.pallas_call(functools.partial(fused_kernel, size), in_specs=[vmem, vme...]
    all_gather x6 -> x4, waiting for transfers between devices: 26.8 us -> 0.03 us  [gather(): return lax.all_gather(shard, 'wsh', axis=axis, tiled=True)]
    pallas_call x2, Pallas kernels: 129 us -> 113 us  [ring_gather(): pl.pallas_call(functools.partial(ring_gather_kernel, size, count), in_spe...]
    dot_general x2 -> x0, local copies, waits for them, and re-layouts: 8.43 us -> none  [dot(): return jnp.dot(a, b, preferred_element_type=F32)]
  transfers between devices with their start and end apart: 10 -> 7, of which waited for: 3 -> 2; matrix products, arithmetic and copies ran while one was open for 12% -> 10% of each run, Pallas kernels for 59% -> 51%
where the time goes in v3:
time: 733 us; the launch traced here: 727 us
  Pallas kernels  513 us (70%)
  waiting for transfers between devices  100 us (14%)
  local copies, waits for them, and re-layouts  47 us (6%)
  matrix products  26.8 us (4%)
  other arithmetic  25.1 us (3%)
  between operations  14.9 us (2%)
    pallas_call x1, Pallas kernels, fused_experts(): pl.pallas_call(functools.partial(fused_kernel, size), in_specs=[vmem, vme...  140 us
    pallas_call x1, Pallas kernels, reduce_grads(): pl.pallas_call(functools.partial(reduce_kernel, size, shards), in_specs=[...  117 us
    pallas_call x2, Pallas kernels, ring_gather(): pl.pallas_call(functools.partial(ring_gather_kernel, size, count), in_spe...  113 us
    reduce_scatter x2, waiting for transfers between devices, scatter(): lax.psum_scatter(grad.astype(BF16), 'wsh', scatter_dimension=dim, tiled=T...  97.9 us
    pallas_call x1, Pallas kernels, ring_scatter(): pl.pallas_call(functools.partial(ring_scatter_kernel, size, count), in_sp...  67.4 us
    pallas_call x1, Pallas kernels, attend_back(): pl.pallas_call(attend_back_kernel, grid=(PAIRS, PAIR_HEADS), in_specs=[he...  41.3 us
    pallas_call x1, Pallas kernels, attend(): pl.pallas_call(attend_kernel, grid=(PAIRS, PAIR_HEADS), in_specs=[head, k...  34.8 us
  transfers between devices with their start and end apart: 7, of which 2 were waited for; matrix products, arithmetic and copies ran while one was open for 10% of the time, Pallas kernels for 51%

profile of v3, /device:TPU:0, one launch (start us, length us, event | category | flops | bytes accessed | tf_op | source)
XLA Modules:
  0.0 727.5 jit_solution(8010274129481264442)
XLA Ops:
  9.5 3.0 fusion.5
  18.2 67.4 %gather_grads.1.g_hbm = bf16[2048,1536]{1,0:T(8,128)(2,1)} custom-call(bf16[256,1536]{1,0:T(8,128)(2,1)} %bitcast.126), custom_call_target="tpu_custom_call" | custom-call | bytes 104857600 | tf_op jit(solution)/shard_map/gather_grads/pallas_call | solution.py:447
  88.5 5.6 fusion.2
  101.0 2.1 copy.72
  104.7 45.2 %gather_keys.1 = (bf16[2048,512]{1,0:T(8,128)(2,1)}, bf16[2048,512]{1,0:T(8,128)(2,1)}) custom-call(bf16[256,512]{1,0:T(8,128)(2,1)} %copy.74.refs_0_, bf16[256,512]{1,0:T(8,128)(2,1)} %slice.199.refs_1_), custom_call_target="tpu_custom_call" | custom-call | bytes 104857600 | tf_op jit(solution)/shard_map/gather_keys/pallas_call | solution.py:447
  150.0 34.8 %attend.1 = (f32[4,6,128,256]{3,2,1,0:T(8,128)}, f32[4,6,1,256]{3,2,1,0:T(1,128)}) custom-call(bf16[4,6,128,256]{3,2,1,0:T(8,128)(2,1)} %copy.75.q_ref, bf16[2048,512]{1,0:T(8,128)(2,1)} %get-tuple-element.33.k_ref, bf16[2048,512]{1,0:T(8,128)(2,1)} %get-tuple-element.34.v_ref, s32[2048,1]{1,0:T(8,128)} %copy.76.kdoc_ref, s32[2048,1]{1,0:T(8,128)} %copy.77.kplace_ref, ...), custom_call_target="tpu_custom_call" | custom-call | flops 6442450944 | bytes 16777216 | tf_op jit(solution)/shard_map/attend/pallas_call | solution.py:190
  188.0 4.4 multiply_reduce_fusion.2
  192.6 1.9 fusion.46
  195.2 139.8 %fused_experts.1 = (f32[256,1536]{1,0:T(8,128)}, f32[16,256]{1,0:T(8,128)}, bf16[2048,1536]{1,0:T(8,128)(2,1)}, bf16[2,1536,1024]{2,1,0:T(8,128)(2,1)}, bf16[2,512,1536]{2,1,0:T(8,128)(2,1)}) custom-call(bf16[256,1536]{1,0:T(8,128)(2,1)} %copy-done.9, f32[16,256]{1,0:T(8,128)} %fusion.41.gate_in, bf16[2048,1536]{1,0:T(8,128)(2,1)} %gather_grads.1.g_hbm, ...), custom_call_target="tpu_custom_call" | custom-call | flops 57982058496 | bytes 314572800 | tf_op jit(solution)/shard_map/fused_experts/pallas_call | solution.py:787
  335.7 36.6 %reduce-scatter.6.cloned.1.call-done = bf16[2,128,1536]{2,1,0:T(8,128)(2,1)} async-done(((bf16[2,512,1536]{2,1,0:T(8,128)(2,1)}), bf16[2,128,1536]{2,1,0:T(8,128)(2,1)}) %reduce-scatter.6.cloned.1.call-update) | async-done | bytes 786448 | tf_op jit(solution)/shard_map/reduce_scatter | solution.py:1178
  372.3 61.3 %reduce-scatter.4.cloned.1.call-done = bf16[2,384,1024]{2,1,0:T(8,128)(2,1)} async-done(((bf16[2,1536,1024]{2,1,0:T(8,128)(2,1)}), bf16[2,384,1024]{2,1,0:T(8,128)(2,1)}) %reduce-scatter.4.cloned.1.call-update) | async-done | bytes 1572880 | tf_op jit(solution)/shard_map/reduce_scatter | solution.py:1178
  435.0 2.3 multiply_reduce_fusion
  442.5 5.1 convolution_convert_fusion
  447.6 2.4 copy.81
  450.0 2.3 convert_multiply_fusion.4
  457.3 41.3 %attend_back.1 = (f32[4,6,128,256]{3,2,1,0:T(8,128)}, bf16[2048,512]{1,0:T(8,128)(2,1)}, bf16[2048,512]{1,0:T(8,128)(2,1)}) custom-call(bf16[4,6,128,256]{3,2,1,0:T(8,128)(2,1)} %copy.75.q_ref, bf16[4,6,256,128]{3,2,1,0:T(8,128)(2,1)} %bitcast.128, bf16[4,6,128,256]{3,2,1,0:T(8,128)(2,1)} %copy.87.g_ref, bf16[4,6,256,128]{3,2,1,0:T(8,128)(2,1)} %bitcast.131, ...), custom_call_target="tpu_custom_call" | custom-call | flops 16106127360 | bytes 25165824 | tf_op jit(solution)/shard_map/attend_back/pallas_call | solution.py:212
  504.3 67.4 %scatter_keys.1 = (f32[256,512]{1,0:T(8,128)S(1)}, f32[256,512]{1,0:T(8,128)S(1)}) custom-call(bf16[2048,512]{1,0:T(8,128)(2,1)S(1)} %copy-done, bf16[2048,512]{1,0:T(8,128)(2,1)S(1)} %copy-done.1), custom_call_target="tpu_custom_call" | custom-call | bytes 104857600 | tf_op jit(solution)/shard_map/scatter_keys/pallas_call | solution.py:523
  573.1 5.6 fusion
  582.6 2.5 pad_maximum_fusion.rhs
  585.1 117.1 %reduce_grads.1 = f32[400,4096]{1,0:T(8,128)} custom-call(bf16[2,1536,256]{2,1,0:T(8,128)(2,1)} %copy.96.lhs, bf16[256,4096]{1,0:T(8,128)(2,1)} %pad_maximum_fusion.rhs, bf16[4,16,4096]{2,1,0:T(8,128)(2,1)} %pad.18.small), custom_call_target="tpu_custom_call" | custom-call | flops 3221225472 | bytes 314572800 | tf_op jit(solution)/shard_map/reduce_grads/pallas_call | solution.py:983
  704.2 2.1 convert_element_type.113
  707.7 2.6 fusion.44
  710.3 5.0 fusion.43
  715.9 4.5 fusion.13
  (155 shorter events, 50.3 us)
Async XLA Ops:
  7.2 79.6 %all-gather.5.cloned.1.call-start = ((), (), s32[]{:S(2)}) async-start(), calls=%async_computation.3 | async-start | bytes 10321920 | tf_op jit(solution)/shard_map/all_gather | solution.py:1038
  12.4 2.1 copy-start.27
  12.5 2.3 copy-start.25
  12.5 175.6 %all-gather.7.cloned.1.call-start = ((), (), s32[]{:S(2)}) async-start(), calls=%async_computation.4 | async-start | bytes 5898240 | tf_op jit(solution)/shard_map/all_gather | solution.py:1038
  13.2 182.0 %all-gather.11.cloned.1.call-start = ((), (), s32[]{:S(2)}) async-start(), calls=%async_computation.6 | async-start | bytes 3932160 | tf_op jit(solution)/shard_map/all_gather | solution.py:1038
  14.0 181.3 %all-gather.9.cloned.1.call-start = ((), (), s32[]{:S(2)}) async-start(), calls=%async_computation.5 | async-start | bytes 7864320 | tf_op jit(solution)/shard_map/all_gather | solution.py:1038
  14.5 357.8 %reduce-scatter.6.cloned.1.call-start = ((), (), s32[]{:S(2)}) async-start(), calls=%async_computation.8 | async-start | bytes 3932160 | tf_op jit(solution)/shard_map/reduce_scatter | solution.py:1178
  18.2 68.0 %copy-start.26 = (s32[1,256,8]{1,2,0:T(8,128)S(1)}, s32[1,256,8]{1,2,0:T(8,128)}, u32[]{:S(2)}) copy-start(s32[1,256,8]{1,2,0:T(8,128)} %param.26) | copy-start | bytes 24580
  18.2 68.1 %copy-start.7 = (bf16[1,256,1536]{2,1,0:T(8,128)(2,1)S(1)}, bf16[1,256,1536]{2,1,0:T(8,128)(2,1)}, u32[]{:S(2)}) copy-start(bf16[1,256,1536]{2,1,0:T(8,128)(2,1)} %param.14) | copy-start | bytes 2359300
  103.1 1.7 copy-start.10
  192.4 2.2 copy-start.2
  192.6 2.6 copy-start.9
  335.1 98.5 %reduce-scatter.4.cloned.1.call-start = ((), (), s32[]{:S(2)}) async-start(), calls=%async_computation.7 | async-start | bytes 7864320 | tf_op jit(solution)/shard_map/reduce_scatter | solution.py:1178
  335.7 370.6 %reduce-scatter.8.cloned.1.call-start = ((), (), s32[]{:S(2)}) async-start(), calls=%async_computation.9 | async-start | bytes 7077888 | tf_op jit(solution)/shard_map/reduce_scatter | solution.py:1183
  437.3 4.3 copy-start.5
  447.6 2.4 copy-start.12
  455.6 1.7 copy-start.11
  500.6 2.2 copy-start
  573.1 5.6 copy-start.8
  578.7 2.1 copy-start.15
  585.1 117.2 %copy-start.22 = (bf16[2,128,1536]{2,1,0:T(8,128)(2,1)S(1)}, bf16[2,128,1536]{2,1,0:T(8,128)(2,1)}, u32[]{:S(2)}) copy-start(bf16[2,128,1536]{2,1,0:T(8,128)(2,1)} %reduce-scatter.6.cloned.1.call-done) | copy-start | bytes 2359300
  702.3 2.0 copy-start.21
  710.3 5.7 copy-start.4
  710.3 5.7 copy-start.6
  (11 other events, 13.6 us)
Sparse Core Ops, SparseCore 0:
  12.6 60.2 all-gather.4
  74.4 37.4 all-gather.6
  113.4 28.5 all-gather.10
  143.4 46.3 all-gather.8
  335.2 37.0 reduce-scatter.5
  374.7 58.8 reduce-scatter.3
  437.2 137.8 reduce-scatter.7

commit v4 on v3

--- a/solution.py
+++ b/solution.py
@@ -1152,6 +1152,15 @@
         marks,
     )
     key_grad, value_grad = ring_scatter([key_part, value_part], group_devices, 4, "scatter_keys")
+    def scatter(grad, dim=0):
+        return lax.psum_scatter(grad.astype(BF16), "wsh", scatter_dimension=dim, tiled=True)
+
+    inner_out = scatter(inner_grad, 1)
+    outer_out = scatter(outer_grad, 1)
+    mixed, inner_out, outer_out, key_grad, value_grad = lax.optimization_barrier(
+        (mixed, inner_out, outer_out, key_grad, value_grad)
+    )
+    mixture = lax.psum_scatter(mixed, "ctx", scatter_dimension=0, tiled=True)
     value_grad = value_grad.astype(BF16)
     query_pre_grad = (
         reverse_rotation(
@@ -1174,13 +1183,6 @@
     gain_one_grad, input_back = norm_backward(inputs_f, inverse_one, gain_one, normed_one_grad)
     input_grad = residual_grad + input_back
 
-    def scatter(grad, dim=0):
-        return lax.psum_scatter(grad.astype(BF16), "wsh", scatter_dimension=dim, tiled=True)
-
-    inner_out = scatter(inner_grad, 1)
-    outer_out = scatter(outer_grad, 1)
-    mixed, inner_out, outer_out = lax.optimization_barrier((mixed, inner_out, outer_out))
-    mixture = lax.psum_scatter(mixed, "ctx", scatter_dimension=0, tiled=True)
     shards = lax.axis_size("wsh")
     shard_rows = query_weight.shape[0]
     columns = 2 * query_weight.shape[1] + 2 * key_value_width

time: 733 us -> 636 us (0.87)
  waiting for transfers between devices: 100 us -> 2.54 us
  Pallas kernels: 513 us -> 500 us
  other arithmetic: 25.1 us -> 33.8 us
    reduce_scatter x2, waiting for transfers between devices: 97.9 us -> 0.04 us  [scatter(): lax.psum_scatter(grad.astype(BF16), 'wsh', scatter_dimension=dim, tiled=T...]
    pallas_call x1, Pallas kernels: 67.4 us -> 29.4 us  [ring_scatter(): pl.pallas_call(functools.partial(ring_scatter_kernel, size, count), in_sp...]
    pallas_call x1, Pallas kernels: 117 us -> 142 us  [reduce_grads(): pl.pallas_call(functools.partial(reduce_kernel, size, shards), in_specs=[...]
  transfers between devices with their start and end apart: 7 -> 7, of which waited for: 2 -> 0; matrix products, arithmetic and copies ran while one was open for 10% -> 14% of each run, Pallas kernels for 51% -> 57%
where the time goes in v4:
time: 636 us; the launch traced here: 631 us
  Pallas kernels  500 us (79%)
  local copies, waits for them, and re-layouts  53.4 us (8%)
  other arithmetic  33.8 us (5%)
  matrix products  25.6 us (4%)
  between operations  14.9 us (2%)
    pallas_call x1, Pallas kernels, reduce_grads(): pl.pallas_call(functools.partial(reduce_kernel, size, shards), in_specs=[...  142 us
    pallas_call x1, Pallas kernels, fused_experts(): pl.pallas_call(functools.partial(fused_kernel, size), in_specs=[vmem, vme...  140 us
    pallas_call x2, Pallas kernels, ring_gather(): pl.pallas_call(functools.partial(ring_gather_kernel, size, count), in_spe...  113 us
    pallas_call x1, Pallas kernels, attend_back(): pl.pallas_call(attend_back_kernel, grid=(PAIRS, PAIR_HEADS), in_specs=[he...  41.4 us
    pallas_call x1, Pallas kernels, attend(): pl.pallas_call(attend_kernel, grid=(PAIRS, PAIR_HEADS), in_specs=[head, k...  34.8 us
    pallas_call x1, Pallas kernels, ring_scatter(): pl.pallas_call(functools.partial(ring_scatter_kernel, size, count), in_sp...  29.4 us
  transfers between devices with their start and end apart: 7, of which 0 were waited for; matrix products, arithmetic and copies ran while one was open for 14% of the time, Pallas kernels for 57%

profile of v4, /device:TPU:0, one launch (start us, length us, event | category | flops | bytes accessed | tf_op | source)
XLA Modules:
  0.0 630.7 jit_solution(4962067017962660827)
XLA Ops:
  9.5 3.0 fusion.5
  18.3 67.4 %gather_grads.1.g_hbm = bf16[2048,1536]{1,0:T(8,128)(2,1)} custom-call(bf16[256,1536]{1,0:T(8,128)(2,1)} %bitcast.126), custom_call_target="tpu_custom_call" | custom-call | bytes 104857600 | tf_op jit(solution)/shard_map/gather_grads/pallas_call | solution.py:447
  88.5 5.6 fusion.2
  104.7 45.2 %gather_keys.1 = (bf16[2048,512]{1,0:T(8,128)(2,1)}, bf16[2048,512]{1,0:T(8,128)(2,1)}) custom-call(bf16[256,512]{1,0:T(8,128)(2,1)} %copy.74.refs_0_, bf16[256,512]{1,0:T(8,128)(2,1)} %slice.199.refs_1_), custom_call_target="tpu_custom_call" | custom-call | bytes 104857600 | tf_op jit(solution)/shard_map/gather_keys/pallas_call | solution.py:447
  150.0 34.8 %attend.1 = (f32[4,6,128,256]{3,2,1,0:T(8,128)}, f32[4,6,1,256]{3,2,1,0:T(1,128)}) custom-call(bf16[4,6,128,256]{3,2,1,0:T(8,128)(2,1)} %copy.75.q_ref, bf16[2048,512]{1,0:T(8,128)(2,1)} %get-tuple-element.35.k_ref, bf16[2048,512]{1,0:T(8,128)(2,1)} %get-tuple-element.36.v_ref, s32[2048,1]{1,0:T(8,128)} %copy.76.kdoc_ref, s32[2048,1]{1,0:T(8,128)} %copy.77.kplace_ref, ...), custom_call_target="tpu_custom_call" | custom-call | flops 6442450944 | bytes 16777216 | tf_op jit(solution)/shard_map/attend/pallas_call | solution.py:190
  188.0 4.4 multiply_reduce_fusion.2
  195.2 139.9 %fused_experts.1 = (f32[256,1536]{1,0:T(8,128)}, f32[16,256]{1,0:T(8,128)}, bf16[2048,1536]{1,0:T(8,128)(2,1)}, bf16[2,1536,1024]{2,1,0:T(8,128)(2,1)}, bf16[2,512,1536]{2,1,0:T(8,128)(2,1)}) custom-call(bf16[256,1536]{1,0:T(8,128)(2,1)} %copy-done.9, f32[16,256]{1,0:T(8,128)} %fusion.41.gate_in, bf16[2048,1536]{1,0:T(8,128)(2,1)} %gather_grads.1.g_hbm, ...), custom_call_target="tpu_custom_call" | custom-call | flops 57982058496 | bytes 314572800 | tf_op jit(solution)/shard_map/fused_experts/pallas_call | solution.py:787
  336.6 2.4 multiply_reduce_fusion
  341.6 4.3 convolution_convert_fusion
  349.7 3.0 copy.83
  352.7 2.6 copy.87.g_ref
  355.3 3.6 convert_bitcast_fusion
  358.9 3.1 copy.85
  364.2 41.4 %attend_back.1 = (f32[4,6,128,256]{3,2,1,0:T(8,128)}, bf16[2048,512]{1,0:T(8,128)(2,1)}, bf16[2048,512]{1,0:T(8,128)(2,1)}) custom-call(bf16[4,6,128,256]{3,2,1,0:T(8,128)(2,1)} %copy.75.q_ref, bf16[4,6,256,128]{3,2,1,0:T(8,128)(2,1)} %bitcast.128, bf16[4,6,128,256]{3,2,1,0:T(8,128)(2,1)} %copy.87.g_ref, bf16[4,6,256,128]{3,2,1,0:T(8,128)(2,1)} %bitcast.130, ...), custom_call_target="tpu_custom_call" | custom-call | flops 16106127360 | bytes 25165824 | tf_op jit(solution)/shard_map/attend_back/pallas_call | solution.py:212
  408.9 29.4 %scatter_keys.1 = (f32[256,512]{1,0:T(8,128)S(1)}, f32[256,512]{1,0:T(8,128)S(1)}) custom-call(bf16[2048,512]{1,0:T(8,128)(2,1)S(1)} %copy-done, bf16[2048,512]{1,0:T(8,128)(2,1)S(1)} %copy-done.1), custom_call_target="tpu_custom_call" | custom-call | bytes 104857600 | tf_op jit(solution)/shard_map/scatter_keys/pallas_call | solution.py:523
  446.3 2.5 convert_element_type.114
  448.8 5.7 fusion
  456.9 2.4 pad_maximum_fusion.4
  459.4 2.6 copy.96.lhs
  462.0 3.6 convert_element_type.113
  467.2 142.2 %reduce_grads.1 = f32[400,4096]{1,0:T(8,128)} custom-call(bf16[2,1536,256]{2,1,0:T(8,128)(2,1)} %copy.96.lhs, bf16[256,4096]{1,0:T(8,128)(2,1)} %pad_maximum_fusion.rhs, bf16[4,16,4096]{2,1,0:T(8,128)(2,1)} %pad.18.small), custom_call_target="tpu_custom_call" | custom-call | flops 3221225472 | bytes 314572800 | tf_op jit(solution)/shard_map/reduce_grads/pallas_call | solution.py:983
  610.8 2.6 fusion.44
  613.4 5.0 fusion.43
  619.0 4.7 fusion.13
  (141 shorter events, 54.7 us)
Async XLA Ops:
  7.2 79.6 %all-gather.5.cloned.1.call-start = ((), (), s32[]{:S(2)}) async-start(), calls=%async_computation.3 | async-start | bytes 10321920 | tf_op jit(solution)/shard_map/all_gather | solution.py:1038
  12.4 2.1 copy-start.20
  12.5 2.3 copy-start.18
  12.5 175.6 %all-gather.7.cloned.1.call-start = ((), (), s32[]{:S(2)}) async-start(), calls=%async_computation.4 | async-start | bytes 5898240 | tf_op jit(solution)/shard_map/all_gather | solution.py:1038
  13.2 182.0 %all-gather.11.cloned.1.call-start = ((), (), s32[]{:S(2)}) async-start(), calls=%async_computation.6 | async-start | bytes 3932160 | tf_op jit(solution)/shard_map/all_gather | solution.py:1038
  14.0 181.3 %all-gather.9.cloned.1.call-start = ((), (), s32[]{:S(2)}) async-start(), calls=%async_computation.5 | async-start | bytes 7864320 | tf_op jit(solution)/shard_map/all_gather | solution.py:1038
  14.5 423.7 %reduce-scatter.6.cloned.1.call-start = ((), (), s32[]{:S(2)}) async-start(), calls=%async_computation.8 | async-start | bytes 3932160 | tf_op jit(solution)/shard_map/reduce_scatter | solution.py:1156
  18.3 68.0 %copy-start.19 = (s32[1,256,8]{1,2,0:T(8,128)S(1)}, s32[1,256,8]{1,2,0:T(8,128)}, u32[]{:S(2)}) copy-start(s32[1,256,8]{1,2,0:T(8,128)} %param.26) | copy-start | bytes 24580
  18.3 68.1 %copy-start.5 = (bf16[1,256,1536]{2,1,0:T(8,128)(2,1)S(1)}, bf16[1,256,1536]{2,1,0:T(8,128)(2,1)}, u32[]{:S(2)}) copy-start(bf16[1,256,1536]{2,1,0:T(8,128)(2,1)} %param.14) | copy-start | bytes 2359300
  103.1 1.7 copy-start.10
  192.4 2.2 copy-start.2
  192.6 2.6 copy-start.9
  335.1 103.2 %reduce-scatter.4.cloned.1.call-start = ((), (), s32[]{:S(2)}) async-start(), calls=%async_computation.7 | async-start | bytes 7864320 | tf_op jit(solution)/shard_map/reduce_scatter | solution.py:1156
  335.7 273.7 %reduce-scatter.8.cloned.1.call-start = ((), (), s32[]{:S(2)}) async-start(), calls=%async_computation.9 | async-start | bytes 7077888 | tf_op jit(solution)/shard_map/reduce_scatter | solution.py:1163
  336.6 3.6 copy-start.8
  405.6 1.6 copy-start
  407.2 1.7 copy-start.1
  446.1 2.7 copy-start.14
  448.8 5.7 copy-start.6
  454.5 1.5 copy-start.11
  454.5 2.4 copy-start.13
  462.0 3.6 copy-start.12
  462.0 3.6 copy-start.16
  613.4 5.6 copy-start.7
  (4 other events, 4.2 us)
Sparse Core Ops, SparseCore 0:
  12.6 60.2 all-gather.4
  74.4 37.4 all-gather.6
  113.4 28.4 all-gather.10
  143.4 46.3 all-gather.8
  335.3 36.7 reduce-scatter.5
  374.4 58.8 reduce-scatter.3
  438.5 145.6 reduce-scatter.7
